TPU v7x, 32 devices: a whole 2x2x4 slice. The times are simulated.
32 devices in a mesh: sec: 8 (over z, y), tile: 4 (over x, core).
Axes of the slice: x: 2, y: 2, z: 4, core: 2. Of those that a mesh axis runs over, the one named last changes fastest.
Arguments:
- patches: bfloat16 [48, 8, 8, 128, 128], P('sec', 'tile'), may hold values from -6 to 6
- pair_flags: int32 [48, 3], P('sec'), may hold values 0 or 1
- nodes: float32 [2, 48, 8, 8], P(None, 'sec', 'tile'), may hold values from -6 to 6
Outputs:
- relaxed: float32 [2, 48, 8, 8], P(None, 'sec', 'tile')
- measured: float32 [2, 48, 3, 8, 8], P(None, 'sec', None, 'tile')
Inputs may be any that keep to these rules, and one draw needn't show every extreme that they name: `pair_flags`: flags of pairs whose partner lies past the last section are ignored.
All inputs are finite; a program needn't handle non-finite values. No bound on the sum of `pair_flags` on one device may be relied on, other than what follows from the above.
Results may differ from a plain program's by a relative error of at most 0.0081.
Values may be sent and summed in bfloat16 or wider, within the bound.
A program may use at most 128 MiB of HBM per device.

v0:
```python
import math

import jax
import jax.numpy as jnp
from jax import lax
from jax.sharding import PartitionSpec as P

SWEEPS = 8


STEP_SIZE = 0.08
EPSILON = 1e-06


def shifted(value, axis, by):
    count = lax.axis_size(axis)
    pairs = [(i, i + by) for i in range(count) if 0 <= i + by < count]
    return lax.ppermute(value, axis, pairs)


def padded(block, sides, width):
    for axis, dim in sides:
        count = lax.axis_size(axis)
        forward = [(i, i + 1) for i in range(count - 1)]
        backward = [(target, source) for source, target in forward]
        low = lax.ppermute(
            lax.slice_in_dim(block, block.shape[dim] - width, None, axis=dim), axis, forward
        )
        high = lax.ppermute(lax.slice_in_dim(block, 0, width, axis=dim), axis, backward)
        block = jnp.concatenate([low, block, high], axis=dim)
    return block


def transform_tables(length):
    index = jnp.arange(length, dtype=jnp.int32)
    phase = (index[:, None] * index[None, :] % length).astype(jnp.float32) * (
        2.0 * math.pi / length
    )
    cosine = jnp.cos(phase)
    sine = jnp.sin(phase)
    forward_first = jnp.concatenate([cosine, sine], axis=1).astype(jnp.bfloat16)
    forward_second = jnp.stack(
        [jnp.stack([cosine, -sine], 1), jnp.stack([-sine, -cosine], 1)], 0
    ).astype(jnp.bfloat16)
    inverse_first = jnp.stack(
        [jnp.stack([cosine, sine], 1), jnp.stack([-sine, cosine], 1)], 0
    ).astype(jnp.bfloat16)
    inverse_second = jnp.stack([cosine, -sine], 1).astype(jnp.bfloat16)
    shifts = jnp.where(index < length // 2, index, index - length).astype(jnp.float32)
    return (forward_first, forward_second, inverse_first, inverse_second, shifts)


def spectrum(block, tabs):
    length = block.shape[-1]
    half = jnp.einsum("...aj,jm->...am", block, tabs[0], preferred_element_type=jnp.float32).astype(
        jnp.bfloat16
    )
    half = half.reshape(half.shape[:-1] + (2, length))
    return jnp.einsum(
        "rahj,...jhk->...rak", tabs[1], half, preferred_element_type=jnp.float32
    ).astype(jnp.bfloat16)


def measure(first_spec, second_spec, weight, tabs):
    length = first_spec.shape[-1]
    left = first_spec.astype(jnp.float32)
    right = second_spec.astype(jnp.float32)
    real = left[..., 0, :, :] * right[..., 0, :, :] + left[..., 1, :, :] * right[..., 1, :, :]
    imag = left[..., 0, :, :] * right[..., 1, :, :] - left[..., 1, :, :] * right[..., 0, :, :]
    cross = jnp.stack([real, imag], axis=-3).astype(jnp.bfloat16)
    back = jnp.einsum(
        "...qaj,qjrk->...rak", cross, tabs[2], preferred_element_type=jnp.float32
    ).astype(jnp.bfloat16)
    corr = jnp.einsum("arj,...rjk->...ak", tabs[3], back, preferred_element_type=jnp.float32) * (
        1.0 / float(length) ** 3
    )
    power = corr * corr
    total = jnp.mean(power, axis=(-2, -1)) + EPSILON
    along_rows = jnp.mean(power * tabs[4][:, None], axis=(-2, -1))
    along_cols = jnp.mean(power * tabs[4][None, :], axis=(-2, -1))
    return jnp.stack([along_rows / total, along_cols / total], 0) * weight


def grid_force(u):
    rows = u.shape[2]
    cols = u.shape[3]
    row_place = jnp.arange(rows, dtype=jnp.int32)
    col_place = jnp.arange(cols, dtype=jnp.int32)
    has_up = (row_place > 0).astype(jnp.float32)[:, None]
    has_down = (row_place < rows - 1).astype(jnp.float32)[:, None]
    has_left = (col_place > 0).astype(jnp.float32)[None, :]
    has_right = (col_place < cols - 1).astype(jnp.float32)[None, :]
    zero_row = jnp.zeros_like(u[:, :, :1])
    zero_col = jnp.zeros_like(u[..., :1])
    above = jnp.concatenate([zero_row, u[:, :, :-1]], axis=2)
    below = jnp.concatenate([u[:, :, 1:], zero_row], axis=2)
    left = jnp.concatenate([zero_col, u[..., :-1]], axis=3)
    right = jnp.concatenate([u[..., 1:], zero_col], axis=3)
    return (
        has_up * (above - u)
        + has_down * (below - u)
        + has_left * (left - u)
        + has_right * (right - u)
    )


def shards(patches, pair_flags, nodes):
    tabs = transform_tables(patches.shape[-1])
    local = patches.shape[0]
    reach = pair_flags.shape[1]
    own = spectrum(patches, tabs)
    received = shifted(patches[:reach], "sec", -1)
    ahead = spectrum(received, tabs)
    extended = jnp.concatenate([own, ahead], axis=0)
    sections = lax.axis_size("sec") * local
    placed = lax.axis_index("sec") * local + jnp.arange(local, dtype=jnp.int32)
    offsets = jnp.arange(1, reach + 1, dtype=jnp.int32)
    weights = pair_flags.astype(jnp.float32) * (
        placed[:, None] + offsets[None, :] < sections
    ).astype(jnp.float32)

    def one_section(items):
        mine, other, weight = items
        return measure(mine, other, weight, tabs)

    columns = []
    for step in range(reach):
        values = lax.map(
            one_section, (own, extended[step + 1 : step + 1 + local], weights[:, step])
        )
        columns.append(jnp.transpose(values, (1, 0, 2, 3)))
    measured = jnp.stack(columns, axis=2)
    rows_local = nodes.shape[2]
    node_full = lax.all_gather(nodes, "tile", axis=2, tiled=True)
    pair_full = lax.all_gather(measured, "tile", axis=3, tiled=True)
    spread_full = jnp.broadcast_to(weights[None, :, :, None, None], (1,) + pair_full.shape[1:])
    stacked_full = jnp.concatenate([pair_full, spread_full], axis=0)
    earlier_full = shifted(stacked_full[:, local - reach :], "sec", 1)
    terms_full = jnp.concatenate([earlier_full, stacked_full], axis=1)
    state = node_full
    for sweep in range(SWEEPS):
        window = padded(state, (("sec", 1),), reach)
        spring = jnp.zeros_like(state)
        for step in range(reach):
            offset = step + 1
            resid = terms_full[2:3, :, step] * (
                window[:, offset : offset + local + reach]
                - window[:, : local + reach]
                - terms_full[:2, :, step]
            )
            spring = spring + resid[:, reach:] - resid[:, reach - offset : reach - offset + local]
        state = state + STEP_SIZE * (grid_force(state) + spring)
    positions = lax.dynamic_slice_in_dim(state, lax.axis_index("tile") * rows_local, rows_local, 2)
    return (positions, measured)


def solution(mesh):
    placed = (P("sec", "tile", None, None, None), P("sec", None), P(None, "sec", "tile", None))
    return jax.shard_map(
        shards,
        mesh=mesh,
        in_specs=placed,
        out_specs=(P(None, "sec", "tile", None), P(None, "sec", None, "tile", None)),
        check_vma=False,
    )
```

profile of v0, /device:TPU:0, one launch (start us, length us, event | category | flops | bytes accessed | tf_op | source)
XLA Modules:
  0.0 266.1 jit_solution(9319691039815945819)
XLA Ops:
  0.6 1.5 slice.520
  3.5 6.2 %all_gather.6 = f32[2,6,8,8]{3,0,1,2:T(2,128)S(1)} all-gather(f32[2,6,2,8]{3,0,1,2:T(2,128)S(1)} %copy.39), channel_id=1, replica_groups=mesh['sec'=8,'tile'=4] {'tile'}, dimensions={2}, use_global_device_ids=true | all-gather | bytes 3840 | tf_op jit(solution)/shard_map/all_gather | solution.py:134
  9.9 4.5 %collective-permute-start.2 = (f32[2,3,8,8]{1,3,2,0:T(8,128)S(1)}, f32[2,3,8,8]{1,3,2,0:T(8,128)S(1)}, u32[]{:S(2)}, u32[]{:S(2)}) collective-permute-start(f32[2,3,8,8]{1,3,2,0:T(8,128)S(1)} %get-tuple-element.470), channel_id=1, source_target_pairs={{0,4},{4,8},{8,12},{12,16},{16,20},{20,24},{24,28},{1,5},{5,9},{9,... | collective-permute-start | bytes 4616 | tf_op jit(solution)/shard_map/ppermute | solution.py:26
  17.0 3.7 %convolution_convert_fusion = bf16[256,6,2,8,128]{4,0,3,2,1:T(8,128)(2,1)S(1)} fusion(bf16[6,2,8,128,128]{4,3,2,1,0:T(8,128)(2,1)} %param.9, bf16[128,128]{0,1:T(8,128)(2,1)S(1)} %get-tuple-element.478, bf16[128,128]{0,1:T(8,128)(2,1)S(1)} %get-tuple-element.479), kind=kOutput, calls=%fused_computation.100 | convolution fusion | flops 808583168 | bytes 9502720 | tf_op jit(solution)/shard_map/...aj,jm->...am/dot_general | solution.py:55
  20.7 4.0 %fusion.62 = bf16[6,2,8,2,128,128]{4,5,3,2,1,0:T(8,128)(2,1)} fusion(bf16[6,2,8,128,2,128,1]{3,5,4,6,2,1,0:T(8,128)(2,1)S(1)} %bitcast.377, bf16[1,128,2,128]{3,1,2,0:T(8,128)(2,1)S(1)} %get-tuple-element.474, bf16[1,128,2,128]{3,1,2,0:T(8,128)(2,1)S(1)} %fusion.195), kind=kOutput, calls=%fused_computation.97 | convolution fusion | flops 1614020608 | bytes 12713984 | tf_op jit(solution)/shard_map/rahj,...jhk->...rak/dot_general | solution.py:59
  24.6 8.7 %copy.48 = bf16[6,2,8,2,128,128]{5,4,3,2,1,0:T(8,128)(2,1)} copy(bf16[6,2,8,2,128,128]{4,5,3,2,1,0:T(8,128)(2,1)} %fusion.62) | data formatting | bytes 12582912
  33.5 8.7 %collective-permute-done = bf16[3,2,8,128,128]{4,3,2,1,0:T(8,128)(2,1)} collective-permute-done((bf16[3,2,8,128,128]{4,3,2,1,0:T(8,128)(2,1)S(1)}, bf16[3,2,8,128,128]{4,3,2,1,0:T(8,128)(2,1)}, u32[]{:S(2)}, u32[]{:S(2)}) %collective-permute-start) | collective-permute-done | bytes 1572896 | tf_op jit(solution)/shard_map/ppermute | solution.py:18
  42.3 2.4 convolution_convert_fusion.1
  45.7 1.8 copy-done
  47.4 6.8 %fusion.61 = (bf16[6,2,8,2,128,128]{4,5,3,2,1,0:T(8,128)(2,1)}, bf16[6,2,8,2,128,128]{4,5,3,2,1,0:T(8,128)(2,1)}, bf16[6,2,8,2,128,128]{4,5,3,2,1,0:T(8,128)(2,1)}) fusion(bf16[6,2,8,2,128,128]{4,5,3,2,1,0:T(8,128)(2,1)S(1)} %copy-done, bf16[3,2,8,2,128,128]{4,5,3,2,1,0:T(8,128)(2,1)S(1)} %fusion.63), kind=kLoop, calls=%fused_computation.96 | loop fusion | flops 9437184 | bytes 28311552 | tf_op jit(solution)/shard_map/concatenate | solution.py:114
  54.2 39.3 %while.36 = (s32[]{:T(128)}, f32[6,2,2,8]{3,1,0,2:T(2,128)S(1)}, bf16[6,2,8,2,128,128]{5,4,3,2,1,0:T(8,128)(2,1)}, bf16[6,2,8,2,128,128]{4,5,3,2,1,0:T(8,128)(2,...) while((s32[]{:T(128)}, f32[6,2,2,8]{3,1,0,2:T(2,128)S(1)}, ...), condition=%wide.region_4.5_spmd.clone.clone, body=%wide.region_0.4_spmd.clone.clone.sunk | while | flops 410256032 | bytes 16979824 | solution.py:128
  56.2 1.7 bitcast_convert_fusion.14
  62.8 1.7 bitcast_convert_fusion.14
  69.3 1.7 bitcast_convert_fusion.14
  75.9 1.7 bitcast_convert_fusion.14
  82.4 1.7 bitcast_convert_fusion.14
  89.0 1.7 bitcast_convert_fusion.14
  93.6 38.5 %while.37 = (s32[]{:T(128)}, f32[6,2,2,8]{3,1,0,2:T(2,128)S(1)}, bf16[6,2,8,2,128,128]{5,4,3,2,1,0:T(8,128)(2,1)}, bf16[6,2,8,2,128,128]{4,5,3,2,1,0:T(8,128)(2,...) while((s32[]{:T(128)}, f32[6,2,2,8]{3,1,0,2:T(2,128)S(1)}, ...), condition=%wide.region_9.10_spmd.clone.clone, body=%wide.region_5.9_spmd.clone.clone.sunk | while | flops 410256032 | bytes 16979824 | solution.py:128
  95.6 1.7 bitcast_convert_fusion.15
  102.0 1.7 bitcast_convert_fusion.15
  108.4 1.7 bitcast_convert_fusion.15
  114.8 1.7 bitcast_convert_fusion.15
  121.2 1.7 bitcast_convert_fusion.15
  127.7 1.7 bitcast_convert_fusion.15
  132.1 38.6 %while.38 = (s32[]{:T(128)}, f32[6,2,2,8]{3,1,0,2:T(2,128)S(1)}, bf16[6,2,8,2,128,128]{5,4,3,2,1,0:T(8,128)(2,1)}, bf16[6,2,8,2,128,128]{4,5,3,2,1,0:T(8,128)(2,...) while((s32[]{:T(128)}, f32[6,2,2,8]{3,1,0,2:T(2,128)S(1)}, ...), condition=%wide.region_14.15_spmd.clone.clone, body=%wide.region_10.14_spmd.clone.clone.sunk | while | flops 410256032 | bytes 16979824 | solution.py:128
  134.1 1.7 bitcast_convert_fusion.16
  140.5 1.7 bitcast_convert_fusion.16
  147.0 1.7 bitcast_convert_fusion.16
  153.4 1.7 bitcast_convert_fusion.16
  159.8 1.7 bitcast_convert_fusion.16
  166.3 1.7 bitcast_convert_fusion.16
  170.8 5.5 %all_gather.7 = f32[2,6,3,8,8]{4,0,2,1,3:T(2,128)S(1)} all-gather(f32[2,6,3,2,8]{4,0,2,1,3:T(2,128)S(1)} %pad_maximum_fusion.21), channel_id=1, replica_groups=mesh['sec'=8,'tile'=4] {'tile'}, dimensions={3}, use_global_device_ids=true | all-gather | bytes 11520 | tf_op jit(solution)/shard_map/all_gather | solution.py:135
  176.7 4.7 %collective-permute-start.1 = (f32[3,3,3,8,8]{1,4,3,2,0:T(8,128)S(1)}, f32[3,3,3,8,8]{1,4,3,2,0:T(8,128)S(1)}, u32[]{:S(2)}, u32[]{:S(2)}) collective-permute-start(f32[3,3,3,8,8]{1,4,3,2,0:T(8,128)S(1)} %pad_maximum_fusion.1), channel_id=1, source_target_pairs={{0,4},{4,8},{8,12},{12,16},{16,20},{20,24},{24,28},{1,5},{5,9},{9,... | collective-permute-start | bytes 20744 | tf_op jit(solution)/shard_map/ppermute | solution.py:18
  182.2 6.0 %collective-permute-done.1 = f32[3,3,3,8,8]{1,4,3,2,0:T(8,128)S(1)} collective-permute-done((f32[3,3,3,8,8]{1,4,3,2,0:T(8,128)S(1)}, f32[3,3,3,8,8]{1,4,3,2,0:T(8,128)S(1)}, u32[]{:S(2)}, u32[]{:S(2)}) %collective-permute-start.1) | collective-permute-done | bytes 6944 | tf_op jit(solution)/shard_map/ppermute | solution.py:18
  188.9 4.4 %collective-permute-start.4 = (f32[2,3,8,8]{1,3,2,0:T(8,128)S(1)}, f32[2,3,8,8]{1,3,2,0:T(8,128)S(1)}, u32[]{:S(2)}, u32[]{:S(2)}) collective-permute-start(f32[2,3,8,8]{1,3,2,0:T(8,128)S(1)} %get-tuple-element.464), channel_id=1, source_target_pairs={{0,4},{4,8},{8,12},{12,16},{16,20},{20,24},{24,28},{1,5},{5,9},{9,... | collective-permute-start | bytes 4616 | tf_op jit(solution)/shard_map/ppermute | solution.py:26
  195.2 5.1 %collective-permute-done.5 = f32[2,3,8,8]{1,3,2,0:T(8,128)S(1)} collective-permute-done((f32[2,3,8,8]{1,3,2,0:T(8,128)S(1)}, f32[2,3,8,8]{1,3,2,0:T(8,128)S(1)}, u32[]{:S(2)}, u32[]{:S(2)}) %collective-permute-start.5) | collective-permute-done | bytes 1568 | tf_op jit(solution)/shard_map/ppermute | solution.py:29
  200.9 4.8 %collective-permute-start.6 = (f32[2,3,8,8]{1,3,2,0:T(8,128)S(1)}, f32[2,3,8,8]{1,3,2,0:T(8,128)S(1)}, u32[]{:S(2)}, u32[]{:S(2)}) collective-permute-start(f32[2,3,8,8]{1,3,2,0:T(8,128)S(1)} %get-tuple-element.458), channel_id=1, source_target_pairs={{0,4},{4,8},{8,12},{12,16},{16,20},{20,24},{24,28},{1,5},{5,9},{9,... | collective-permute-start | bytes 4616 | tf_op jit(solution)/shard_map/ppermute | solution.py:26
  208.2 3.7 %collective-permute-done.7 = f32[2,3,8,8]{1,3,2,0:T(8,128)S(1)} collective-permute-done((f32[2,3,8,8]{1,3,2,0:T(8,128)S(1)}, f32[2,3,8,8]{1,3,2,0:T(8,128)S(1)}, u32[]{:S(2)}, u32[]{:S(2)}) %collective-permute-start.7) | collective-permute-done | bytes 1568 | tf_op jit(solution)/shard_map/ppermute | solution.py:29
  212.4 2.9 %collective-permute-start.8 = (f32[2,3,8,8]{1,3,2,0:T(8,128)S(1)}, f32[2,3,8,8]{1,3,2,0:T(8,128)S(1)}, u32[]{:S(2)}, u32[]{:S(2)}) collective-permute-start(f32[2,3,8,8]{1,3,2,0:T(8,128)S(1)} %get-tuple-element.452), channel_id=1, source_target_pairs={{0,4},{4,8},{8,12},{12,16},{16,20},{20,24},{24,28},{1,5},{5,9},{9,... | collective-permute-start | bytes 4616 | tf_op jit(solution)/shard_map/ppermute | solution.py:26
  217.8 3.7 %collective-permute-done.9 = f32[2,3,8,8]{1,3,2,0:T(8,128)S(1)} collective-permute-done((f32[2,3,8,8]{1,3,2,0:T(8,128)S(1)}, f32[2,3,8,8]{1,3,2,0:T(8,128)S(1)}, u32[]{:S(2)}, u32[]{:S(2)}) %collective-permute-start.9) | collective-permute-done | bytes 1568 | tf_op jit(solution)/shard_map/ppermute | solution.py:29
  222.1 4.8 %collective-permute-start.10 = (f32[2,3,8,8]{1,3,2,0:T(8,128)S(1)}, f32[2,3,8,8]{1,3,2,0:T(8,128)S(1)}, u32[]{:S(2)}, u32[]{:S(2)}) collective-permute-start(f32[2,3,8,8]{1,3,2,0:T(8,128)S(1)} %get-tuple-element.446), channel_id=1, source_target_pairs={{0,4},{4,8},{8,12},{12,16},{16,20},{20,24},{24,28},{1,5},{5,9},{9,... | collective-permute-start | bytes 4616 | tf_op jit(solution)/shard_map/ppermute | solution.py:26
  228.8 4.3 %collective-permute-done.11 = f32[2,3,8,8]{1,3,2,0:T(8,128)S(1)} collective-permute-done((f32[2,3,8,8]{1,3,2,0:T(8,128)S(1)}, f32[2,3,8,8]{1,3,2,0:T(8,128)S(1)}, u32[]{:S(2)}, u32[]{:S(2)}) %collective-permute-start.11) | collective-permute-done | bytes 1568 | tf_op jit(solution)/shard_map/ppermute | solution.py:29
  233.6 3.0 %collective-permute-start.12 = (f32[2,3,8,8]{1,3,2,0:T(8,128)S(1)}, f32[2,3,8,8]{1,3,2,0:T(8,128)S(1)}, u32[]{:S(2)}, u32[]{:S(2)}) collective-permute-start(f32[2,3,8,8]{1,3,2,0:T(8,128)S(1)} %get-tuple-element.440), channel_id=1, source_target_pairs={{0,4},{4,8},{8,12},{12,16},{16,20},{20,24},{24,28},{1,5},{5,9},{9,... | collective-permute-start | bytes 4616 | tf_op jit(solution)/shard_map/ppermute | solution.py:26
  238.5 4.9 %collective-permute-done.13 = f32[2,3,8,8]{1,3,2,0:T(8,128)S(1)} collective-permute-done((f32[2,3,8,8]{1,3,2,0:T(8,128)S(1)}, f32[2,3,8,8]{1,3,2,0:T(8,128)S(1)}, u32[]{:S(2)}, u32[]{:S(2)}) %collective-permute-start.13) | collective-permute-done | bytes 1568 | tf_op jit(solution)/shard_map/ppermute | solution.py:29
  244.0 5.2 %collective-permute-start.14 = (f32[2,3,8,8]{1,3,2,0:T(8,128)S(1)}, f32[2,3,8,8]{1,3,2,0:T(8,128)S(1)}, u32[]{:S(2)}, u32[]{:S(2)}) collective-permute-start(f32[2,3,8,8]{1,3,2,0:T(8,128)S(1)} %get-tuple-element.434), channel_id=1, source_target_pairs={{0,4},{4,8},{8,12},{12,16},{16,20},{20,24},{24,28},{1,5},{5,9},{9,... | collective-permute-start | bytes 4616 | tf_op jit(solution)/shard_map/ppermute | solution.py:26
  251.1 4.3 %collective-permute-done.15 = f32[2,3,8,8]{1,3,2,0:T(8,128)S(1)} collective-permute-done((f32[2,3,8,8]{1,3,2,0:T(8,128)S(1)}, f32[2,3,8,8]{1,3,2,0:T(8,128)S(1)}, u32[]{:S(2)}, u32[]{:S(2)}) %collective-permute-start.15) | collective-permute-done | bytes 1568 | tf_op jit(solution)/shard_map/ppermute | solution.py:29
  255.9 2.8 %collective-permute-start.16 = (f32[2,3,8,8]{1,3,2,0:T(8,128)S(1)}, f32[2,3,8,8]{1,3,2,0:T(8,128)S(1)}, u32[]{:S(2)}, u32[]{:S(2)}) collective-permute-start(f32[2,3,8,8]{1,3,2,0:T(8,128)S(1)} %get-tuple-element.428), channel_id=1, source_target_pairs={{0,4},{4,8},{8,12},{12,16},{16,20},{20,24},{24,28},{1,5},{5,9},{9,... | collective-permute-start | bytes 4616 | tf_op jit(solution)/shard_map/ppermute | solution.py:26
  260.6 4.3 %collective-permute-done.17 = f32[2,3,8,8]{1,3,2,0:T(8,128)S(1)} collective-permute-done((f32[2,3,8,8]{1,3,2,0:T(8,128)S(1)}, f32[2,3,8,8]{1,3,2,0:T(8,128)S(1)}, u32[]{:S(2)}, u32[]{:S(2)}) %collective-permute-start.17) | collective-permute-done | bytes 1568 | tf_op jit(solution)/shard_map/ppermute | solution.py:29
  (265 shorter events, 109.9 us)
Async XLA Ops:
  0.6 2.8 %copy-start.1 = (f32[2,6,2,8]{3,2,1,0:T(2,128)S(1)}, f32[2,6,2,8]{3,2,1,0:T(2,128)}, u32[]{:S(2)}) copy-start(f32[2,6,2,8]{3,2,1,0:T(2,128)} %param.11) | copy-start | bytes 2308
  2.2 40.1 %collective-permute-start = (bf16[3,2,8,128,128]{4,3,2,1,0:T(8,128)(2,1)S(1)}, bf16[3,2,8,128,128]{4,3,2,1,0:T(8,128)(2,1)}, u32[]{:S(2)}, u32[]{:S(2)}) collective-permute-start(bf16[3,2,8,128,128]{4,3,2,1,0:T(8,128)(2,1)S(1)} %slice.520), channel_id=1, source_target_pairs={{4,0},{8,4},{12,8},{16,12},{20,16},{24,20},{28,24},{5,1},{9,5},{13... | collective-permute-start | bytes 4718600 | tf_op jit(solution)/shard_map/ppermute | solution.py:18
  9.9 171.5 %collective-permute-start.2 = (f32[2,3,8,8]{1,3,2,0:T(8,128)S(1)}, f32[2,3,8,8]{1,3,2,0:T(8,128)S(1)}, u32[]{:S(2)}, u32[]{:S(2)}) collective-permute-start(f32[2,3,8,8]{1,3,2,0:T(8,128)S(1)} %get-tuple-element.470), channel_id=1, source_target_pairs={{0,4},{4,8},{8,12},{12,16},{16,20},{20,24},{24,28},{1,5},{5,9},{9,... | collective-permute-start | bytes 4616 | tf_op jit(solution)/shard_map/ppermute | solution.py:26
  14.5 166.9 %collective-permute-start.3 = (f32[2,3,8,8]{1,3,2,0:T(8,128)S(1)}, f32[2,3,8,8]{1,3,2,0:T(8,128)S(1)}, u32[]{:S(2)}, u32[]{:S(2)}) collective-permute-start(f32[2,3,8,8]{1,3,2,0:T(8,128)S(1)} %get-tuple-element.471), channel_id=1, source_target_pairs={{4,0},{8,4},{12,8},{16,12},{20,16},{24,20},{28,24},{5,1},{9,5},{13... | collective-permute-start | bytes 4616 | tf_op jit(solution)/shard_map/ppermute | solution.py:29
  24.6 8.8 %copy-start.2 = (s32[6,3]{0,1:T(4,128)S(1)}, s32[6,3]{0,1:T(4,128)}, u32[]{:S(2)}) copy-start(s32[6,3]{0,1:T(4,128)} %param.10) | copy-start | bytes 220
  44.6 2.8 %copy-start = (bf16[6,2,8,2,128,128]{4,5,3,2,1,0:T(8,128)(2,1)S(1)}, bf16[6,2,8,2,128,128]{4,5,3,2,1,0:T(8,128)(2,1)}, u32[]{:S(2)}) copy-start(bf16[6,2,8,2,128,128]{4,5,3,2,1,0:T(8,128)(2,1)} %fusion.62) | copy-start | bytes 18874372
  176.7 11.4 %collective-permute-start.1 = (f32[3,3,3,8,8]{1,4,3,2,0:T(8,128)S(1)}, f32[3,3,3,8,8]{1,4,3,2,0:T(8,128)S(1)}, u32[]{:S(2)}, u32[]{:S(2)}) collective-permute-start(f32[3,3,3,8,8]{1,4,3,2,0:T(8,128)S(1)} %pad_maximum_fusion.1), channel_id=1, source_target_pairs={{0,4},{4,8},{8,12},{12,16},{16,20},{20,24},{24,28},{1,5},{5,9},{9,... | collective-permute-start | bytes 20744 | tf_op jit(solution)/shard_map/ppermute | solution.py:18
  188.9 6.3 %collective-permute-start.4 = (f32[2,3,8,8]{1,3,2,0:T(8,128)S(1)}, f32[2,3,8,8]{1,3,2,0:T(8,128)S(1)}, u32[]{:S(2)}, u32[]{:S(2)}) collective-permute-start(f32[2,3,8,8]{1,3,2,0:T(8,128)S(1)} %get-tuple-element.464), channel_id=1, source_target_pairs={{0,4},{4,8},{8,12},{12,16},{16,20},{20,24},{24,28},{1,5},{5,9},{9,... | collective-permute-start | bytes 4616 | tf_op jit(solution)/shard_map/ppermute | solution.py:26
  193.3 7.0 %collective-permute-start.5 = (f32[2,3,8,8]{1,3,2,0:T(8,128)S(1)}, f32[2,3,8,8]{1,3,2,0:T(8,128)S(1)}, u32[]{:S(2)}, u32[]{:S(2)}) collective-permute-start(f32[2,3,8,8]{1,3,2,0:T(8,128)S(1)} %get-tuple-element.465), channel_id=1, source_target_pairs={{4,0},{8,4},{12,8},{16,12},{20,16},{24,20},{28,24},{5,1},{9,5},{13... | collective-permute-start | bytes 4616 | tf_op jit(solution)/shard_map/ppermute | solution.py:29
  200.9 7.3 %collective-permute-start.6 = (f32[2,3,8,8]{1,3,2,0:T(8,128)S(1)}, f32[2,3,8,8]{1,3,2,0:T(8,128)S(1)}, u32[]{:S(2)}, u32[]{:S(2)}) collective-permute-start(f32[2,3,8,8]{1,3,2,0:T(8,128)S(1)} %get-tuple-element.458), channel_id=1, source_target_pairs={{0,4},{4,8},{8,12},{12,16},{16,20},{20,24},{24,28},{1,5},{5,9},{9,... | collective-permute-start | bytes 4616 | tf_op jit(solution)/shard_map/ppermute | solution.py:26
  205.7 6.2 %collective-permute-start.7 = (f32[2,3,8,8]{1,3,2,0:T(8,128)S(1)}, f32[2,3,8,8]{1,3,2,0:T(8,128)S(1)}, u32[]{:S(2)}, u32[]{:S(2)}) collective-permute-start(f32[2,3,8,8]{1,3,2,0:T(8,128)S(1)} %get-tuple-element.459), channel_id=1, source_target_pairs={{4,0},{8,4},{12,8},{16,12},{20,16},{24,20},{28,24},{5,1},{9,5},{13... | collective-permute-start | bytes 4616 | tf_op jit(solution)/shard_map/ppermute | solution.py:29
  212.4 5.4 %collective-permute-start.8 = (f32[2,3,8,8]{1,3,2,0:T(8,128)S(1)}, f32[2,3,8,8]{1,3,2,0:T(8,128)S(1)}, u32[]{:S(2)}, u32[]{:S(2)}) collective-permute-start(f32[2,3,8,8]{1,3,2,0:T(8,128)S(1)} %get-tuple-element.452), channel_id=1, source_target_pairs={{0,4},{4,8},{8,12},{12,16},{16,20},{20,24},{24,28},{1,5},{5,9},{9,... | collective-permute-start | bytes 4616 | tf_op jit(solution)/shard_map/ppermute | solution.py:26
  215.3 6.2 %collective-permute-start.9 = (f32[2,3,8,8]{1,3,2,0:T(8,128)S(1)}, f32[2,3,8,8]{1,3,2,0:T(8,128)S(1)}, u32[]{:S(2)}, u32[]{:S(2)}) collective-permute-start(f32[2,3,8,8]{1,3,2,0:T(8,128)S(1)} %get-tuple-element.453), channel_id=1, source_target_pairs={{4,0},{8,4},{12,8},{16,12},{20,16},{24,20},{28,24},{5,1},{9,5},{13... | collective-permute-start | bytes 4616 | tf_op jit(solution)/shard_map/ppermute | solution.py:29
  222.1 6.7 %collective-permute-start.10 = (f32[2,3,8,8]{1,3,2,0:T(8,128)S(1)}, f32[2,3,8,8]{1,3,2,0:T(8,128)S(1)}, u32[]{:S(2)}, u32[]{:S(2)}) collective-permute-start(f32[2,3,8,8]{1,3,2,0:T(8,128)S(1)} %get-tuple-element.446), channel_id=1, source_target_pairs={{0,4},{4,8},{8,12},{12,16},{16,20},{20,24},{24,28},{1,5},{5,9},{9,... | collective-permute-start | bytes 4616 | tf_op jit(solution)/shard_map/ppermute | solution.py:26
  226.9 6.2 %collective-permute-start.11 = (f32[2,3,8,8]{1,3,2,0:T(8,128)S(1)}, f32[2,3,8,8]{1,3,2,0:T(8,128)S(1)}, u32[]{:S(2)}, u32[]{:S(2)}) collective-permute-start(f32[2,3,8,8]{1,3,2,0:T(8,128)S(1)} %get-tuple-element.447), channel_id=1, source_target_pairs={{4,0},{8,4},{12,8},{16,12},{20,16},{24,20},{28,24},{5,1},{9,5},{13... | collective-permute-start | bytes 4616 | tf_op jit(solution)/shard_map/ppermute | solution.py:29
  233.6 4.9 %collective-permute-start.12 = (f32[2,3,8,8]{1,3,2,0:T(8,128)S(1)}, f32[2,3,8,8]{1,3,2,0:T(8,128)S(1)}, u32[]{:S(2)}, u32[]{:S(2)}) collective-permute-start(f32[2,3,8,8]{1,3,2,0:T(8,128)S(1)} %get-tuple-element.440), channel_id=1, source_target_pairs={{0,4},{4,8},{8,12},{12,16},{16,20},{20,24},{24,28},{1,5},{5,9},{9,... | collective-permute-start | bytes 4616 | tf_op jit(solution)/shard_map/ppermute | solution.py:26
  236.6 6.8 %collective-permute-start.13 = (f32[2,3,8,8]{1,3,2,0:T(8,128)S(1)}, f32[2,3,8,8]{1,3,2,0:T(8,128)S(1)}, u32[]{:S(2)}, u32[]{:S(2)}) collective-permute-start(f32[2,3,8,8]{1,3,2,0:T(8,128)S(1)} %get-tuple-element.441), channel_id=1, source_target_pairs={{4,0},{8,4},{12,8},{16,12},{20,16},{24,20},{28,24},{5,1},{9,5},{13... | collective-permute-start | bytes 4616 | tf_op jit(solution)/shard_map/ppermute | solution.py:29
  244.0 7.1 %collective-permute-start.14 = (f32[2,3,8,8]{1,3,2,0:T(8,128)S(1)}, f32[2,3,8,8]{1,3,2,0:T(8,128)S(1)}, u32[]{:S(2)}, u32[]{:S(2)}) collective-permute-start(f32[2,3,8,8]{1,3,2,0:T(8,128)S(1)} %get-tuple-element.434), channel_id=1, source_target_pairs={{0,4},{4,8},{8,12},{12,16},{16,20},{20,24},{24,28},{1,5},{5,9},{9,... | collective-permute-start | bytes 4616 | tf_op jit(solution)/shard_map/ppermute | solution.py:26
  249.2 6.2 %collective-permute-start.15 = (f32[2,3,8,8]{1,3,2,0:T(8,128)S(1)}, f32[2,3,8,8]{1,3,2,0:T(8,128)S(1)}, u32[]{:S(2)}, u32[]{:S(2)}) collective-permute-start(f32[2,3,8,8]{1,3,2,0:T(8,128)S(1)} %get-tuple-element.435), channel_id=1, source_target_pairs={{4,0},{8,4},{12,8},{16,12},{20,16},{24,20},{28,24},{5,1},{9,5},{13... | collective-permute-start | bytes 4616 | tf_op jit(solution)/shard_map/ppermute | solution.py:29
  255.9 4.7 %collective-permute-start.16 = (f32[2,3,8,8]{1,3,2,0:T(8,128)S(1)}, f32[2,3,8,8]{1,3,2,0:T(8,128)S(1)}, u32[]{:S(2)}, u32[]{:S(2)}) collective-permute-start(f32[2,3,8,8]{1,3,2,0:T(8,128)S(1)} %get-tuple-element.428), channel_id=1, source_target_pairs={{0,4},{4,8},{8,12},{12,16},{16,20},{20,24},{24,28},{1,5},{5,9},{9,... | collective-permute-start | bytes 4616 | tf_op jit(solution)/shard_map/ppermute | solution.py:26
  258.7 6.2 %collective-permute-start.17 = (f32[2,3,8,8]{1,3,2,0:T(8,128)S(1)}, f32[2,3,8,8]{1,3,2,0:T(8,128)S(1)}, u32[]{:S(2)}, u32[]{:S(2)}) collective-permute-start(f32[2,3,8,8]{1,3,2,0:T(8,128)S(1)} %get-tuple-element.429), channel_id=1, source_target_pairs={{4,0},{8,4},{12,8},{16,12},{20,16},{24,20},{28,24},{5,1},{9,5},{13... | collective-permute-start | bytes 4616 | tf_op jit(solution)/shard_map/ppermute | solution.py:29
where the time goes:
time: 269 us; the launch traced here: 266 us
  other arithmetic  62.7 us (23%)
  local copies, waits for them, and re-layouts  61.5 us (23%)
  waiting for transfers between devices  50 us (19%)
  starting transfers between devices  48.8 us (18%)
  matrix products  29.1 us (11%)
  blocking collectives  11.7 us (4%)
    dynamic_slice x54, local copies, waits for them, and re-layouts, shards(): lax.map(one_section, (own, extended[step + 1:step + 1 + local], weights[:...  46.5 us
    ppermute x8, starting transfers between devices, padded(): lax.ppermute(lax.slice_in_dim(block, block.shape[dim] - width, None, axis...  32.5 us
    convert_element_type x18, other arithmetic, measure(): right = second_spec.astype(jnp.float32)  31.4 us
    ppermute x8, waiting for transfers between devices, padded(): lax.ppermute(lax.slice_in_dim(block, 0, width, axis=dim), axis, backward)  30.1 us
    dot_general x18, matrix products, measure(): jnp.einsum('arj,...rjk->...ak', tabs[3], back, preferred_element_type=jnp...  18 us
    ppermute x2, waiting for transfers between devices, shifted(): return lax.ppermute(value, axis, pairs)  14.7 us
    unnamed x11, local copies, waits for them, and re-layouts  11.8 us
    mul x18, other arithmetic, measure(): return jnp.stack([along_rows / total, along_cols / total], 0) * weight  11.8 us
  transfers between devices with their start and end apart: 18, of which 16 were waited for; matrix products, arithmetic and copies ran while one was open for 54% of the time, Pallas kernels for 0%

commit v1 on v0

v1 whole, which is shorter than its diff:
```python
import functools
import math

import jax
import jax.numpy as jnp
import numpy as np
from jax import lax
from jax.experimental import pallas as pl
from jax.experimental.pallas import tpu as pltpu
from jax.sharding import PartitionSpec as P

SWEEPS = 8
STEP_SIZE = 0.08
EPSILON = 1e-06
LANES = 128
TILE = 8
MESH = pl.DeviceIdType.MESH


def tables(n):
    h = n // 2
    k = np.arange(n)
    phase = (k[:, None] * k[None, :] % n) * (2.0 * math.pi / n)
    c = np.asarray(np.cos(phase), np.float32).astype(jnp.bfloat16).astype(np.float32)
    s = np.asarray(np.sin(phase), np.float32).astype(jnp.bfloat16).astype(np.float32)
    first = np.concatenate([c, s], 1)
    part = h + TILE
    second = np.zeros((2 * part, 2 * n), np.float32)
    second[: h + 1, :n] = c[: h + 1]
    second[: h + 1, n:] = -s[: h + 1]
    second[part : part + h + 1, :n] = -s[: h + 1]
    second[part : part + h + 1, n:] = -c[: h + 1]
    inverse = np.concatenate([np.concatenate([c, s], 1), np.concatenate([-s, c], 1)], 0)
    order = (np.arange(n) - h) % n
    last = np.zeros((n, n), np.float32)
    last[:, 0] = c[order, 0]
    last[:, 1:h] = 2.0 * c[order, 1:h]
    last[:, h] = c[order, h]
    last[:, h + 1 :] = -2.0 * s[order, 1:h]
    last *= 1.0 / float(n) ** 3
    weigh = np.zeros((TILE, n), np.float32)
    weigh[0] = 1.0
    weigh[1] = np.where(k < h, k, k - n)
    low = lambda a: np.asarray(a).astype(jnp.bfloat16)
    return low(first), low(second), low(inverse), low(last), weigh


def spectra(x, first, second, put):
    cols, n = x.shape[0], x.shape[-1]
    half = jnp.dot(x.reshape(cols * n, n), first, preferred_element_type=jnp.float32)
    half = half.astype(jnp.bfloat16)
    for c in range(0, cols, 2):
        sides = []
        for d in (c, c + 1):
            mine = half[d * n : (d + 1) * n]
            sides.append(jnp.concatenate([mine[:, :n], mine[:, n:]], axis=0))
        spec = jnp.dot(
            second, jnp.concatenate(sides, axis=1), preferred_element_type=jnp.float32
        )
        put(c, spec[:, :n])
        put(c + 1, spec[:, n:])


def pairs(get_a, get_b, cols, n, inverse, last, weigh, sums):
    h = n // 2
    part = h + TILE
    crosses = []
    for c in range(cols):
        a, b = get_a(c), get_b(c)
        ar, ai, br, bi = a[:part], a[part:], b[:part], b[part:]
        real = ar * br + ai * bi
        imag = ar * bi - ai * br
        real_top = real[:TILE] - imag[h:]
        imag_top = imag[:TILE] + real[h:]
        real = jnp.concatenate([real_top, real[TILE:h]], axis=0).astype(jnp.bfloat16)
        imag = jnp.concatenate([imag_top, imag[TILE:h]], axis=0).astype(jnp.bfloat16)
        crosses.append(jnp.concatenate([real, imag], axis=1))
    back = jnp.dot(
        jnp.concatenate(crosses, axis=0), inverse, preferred_element_type=jnp.float32
    ).astype(jnp.bfloat16)
    place = lax.broadcasted_iota(jnp.int32, (TILE, 1), 0).astype(jnp.float32) + float(h)
    for c in range(0, cols, 2):
        sides = []
        for d in (c, c + 1):
            mine = back[d * h : (d + 1) * h]
            sides.append(jnp.concatenate([mine[:, :n], mine[:, n:]], axis=0))
        corr = jnp.dot(last, jnp.concatenate(sides, axis=1), preferred_element_type=jnp.float32)
        power = corr * corr
        total = power[:TILE]
        ramp = total
        for t in range(1, n // TILE):
            total = total + power[t * TILE : (t + 1) * TILE]
            ramp = ramp + total
        shifted = place * total - float(TILE) * ramp
        total = jnp.sum(total, axis=0, keepdims=True)
        shifted = jnp.sum(shifted, axis=0, keepdims=True)
        for d in (0, 1):
            sums[c + d : c + d + 1, :] = shifted[:, d * n : (d + 1) * n]
            sums[cols + c + d : cols + c + d + 1, :] = total[:, d * n : (d + 1) * n]
    return lax.dot_general(
        weigh,
        sums[...],
        (((1,), (1,)), ((), ())),
        precision=lax.Precision.HIGHEST,
        preferred_element_type=jnp.float32,
    )


def own_kernel(reach, x, first, second, inverse, last, weigh, red, tail, spec, sums):
    row = pl.program_id(0)
    step = pl.program_id(1)
    local = pl.num_programs(1)
    cols, n = x.shape[2], x.shape[-1]

    def put(c, value):
        spec[step, c] = value

        @pl.when(step >= local - reach)
        def _():
            tail[jnp.maximum(step - (local - reach), 0), 0, c] = value.astype(tail.dtype)

    spectra(x[0, 0], first[...], second[...], put)

    def body(offset, carry):
        red[step - offset, offset - 1, row] = pairs(
            lambda c: spec[step - offset, c],
            lambda c: spec[step, c],
            cols, n, inverse[...], last[...], weigh[...], sums,
        )
        return carry

    lax.fori_loop(1, jnp.minimum(step, reach) + 1, body, 0)


def far_kernel(count, x, first, second, inverse, last, weigh, *rest):
    own, red, spec, sums = rest[:count], rest[count], rest[count + 1], rest[count + 2]
    cols, n = x.shape[2], x.shape[-1]

    def put(c, value):
        spec[c] = value

    spectra(x[0, 0], first[...], second[...], put)
    for item in range(count):
        red[item, 0] = pairs(
            lambda c: own[item][0, 0, c].astype(jnp.float32),
            lambda c: spec[c],
            cols, n, inverse[...], last[...], weigh[...], sums,
        )


def fixed(array):
    zeros = (0,) * array.ndim
    return pl.BlockSpec(array.shape, lambda *_: zeros)


def cost(patches, pair_count, n):
    return pl.CostEstimate(
        flops=(patches + pair_count) * 24 * n**3,
        bytes_accessed=patches * n * n * 16,
        transcendentals=0,
    )


def relax_kernel(sizes, base, out, slots, field, weight, send, recv):
    groups, tiles, local, reach, span, grid_rows, grid_cols = sizes
    half = LANES // 2
    sec = lax.axis_index("sec")
    tile = lax.axis_index("tile")
    me = sec * tiles + tile
    count = groups * tiles

    def place(index):
        return (index // tiles, index % tiles)

    barrier = pltpu.get_barrier_semaphore()

    def greet(d, carry):
        pl.semaphore_signal(
            barrier, inc=1, device_id=place((me + d) % count), device_id_type=MESH
        )
        return carry

    lax.fori_loop(1, count, greet, 0)
    pl.semaphore_wait(barrier, count - 1)

    def copy(slot, peer):
        return pltpu.make_async_remote_copy(
            src_ref=base,
            dst_ref=slots.at[slot],
            send_sem=send.at[peer],
            recv_sem=recv.at[slot],
            device_id=place(peer),
            device_id_type=MESH,
        )

    def start(d, carry):
        copy(me, (me + d) % count).start()
        return carry

    lax.fori_loop(1, count, start, 0)
    slots[me] = base[...]

    def finish(d, carry):
        peer = (me + d) % count
        copy(peer, peer).wait_recv()
        copy(me, peer).wait_send()
        return carry

    lax.fori_loop(1, count, finish, 0)

    lane = lax.broadcasted_iota(jnp.int32, (TILE, LANES), 1)
    sub = lax.broadcasted_iota(jnp.int32, (TILE, LANES), 0)
    owner = lane % half // span
    for g in range(groups):
        blocks = [slots[g * tiles + t] for t in range(tiles)]
        for v in range(reach + 1):
            value = jnp.zeros((TILE, LANES), jnp.float32)
            for t in range(tiles):
                moved = blocks[t]
                if t != v:
                    moved = pltpu.roll(moved, (t - v) * span % LANES, 1)
                value = jnp.where(owner == t, moved, value)
            field[v, g * local : (g + 1) * local, :] = value[:local]
        row = jnp.broadcast_to(blocks[0][local : local + 1], (TILE, LANES))
        for v in range(reach):
            w = jnp.sum(jnp.where(lane == sub * reach + v, row, 0.0), axis=1, keepdims=True)
            w = jnp.broadcast_to(w, (TILE, LANES))
            weight[v, g * local : (g + 1) * local, :] = w[:local]

    total = groups * local
    spot = lax.broadcasted_iota(jnp.int32, (total, LANES), 1) % half
    across = spot % grid_cols
    down = spot // grid_cols
    one = lambda mask: mask.astype(jnp.float32)
    left, right = one(across > 0), one(across < grid_cols - 1)
    up, below = one(down > 0), one(down < grid_rows - 1)

    def sweep(_, u):
        plane = (
            up * (pltpu.roll(u, grid_cols, 1) - u)
            + below * (pltpu.roll(u, LANES - grid_cols, 1) - u)
            + left * (pltpu.roll(u, 1, 1) - u)
            + right * (pltpu.roll(u, LANES - 1, 1) - u)
        )
        spring = jnp.zeros_like(u)
        for v in range(reach):
            o = v + 1
            r = weight[v] * (pltpu.roll(u, total - o, 0) - u - field[v])
            spring = spring + r - pltpu.roll(r, o, 0)
        return u + STEP_SIZE * (plane + spring)

    state = lax.fori_loop(0, SWEEPS, sweep, field[reach])
    field[reach] = state
    mine = field[reach, pl.ds(sec * local, local), :]
    mine = jnp.concatenate([mine, jnp.zeros((TILE - local, LANES), jnp.float32)], axis=0)
    out[...] = pltpu.roll(mine, (LANES - tile * span) % LANES, 1)


def shards(patches, pair_flags, nodes):
    local, rows, cols, n = patches.shape[:4]
    reach = pair_flags.shape[1]
    groups, tiles = lax.axis_size("sec"), lax.axis_size("tile")
    part = n // 2 + TILE
    tabs = [jnp.asarray(t) for t in tables(n)]
    tab_specs = [fixed(t) for t in tabs]
    back_by_one = [(i, i - 1) for i in range(1, groups)]
    ahead = [lax.ppermute(patches[r : r + 1], "sec", back_by_one) for r in range(reach)]

    patch_block = (1, 1, cols, n, n)
    red, tail = pl.pallas_call(
        functools.partial(own_kernel, reach),
        grid=(rows, local),
        in_specs=[pl.BlockSpec(patch_block, lambda i, s: (s, i, 0, 0, 0))] + tab_specs,
        out_specs=[
            pl.BlockSpec((local, reach, rows, TILE, 2 * cols), lambda i, s: (0, 0, 0, 0, 0)),
            pl.BlockSpec((reach, 1, cols, 2 * part, n), lambda i, s: (0, i, 0, 0, 0)),
        ],
        out_shape=[
            jax.ShapeDtypeStruct((local, reach, rows, TILE, 2 * cols), jnp.float32),
            jax.ShapeDtypeStruct((reach, rows, cols, 2 * part, n), jnp.bfloat16),
        ],
        scratch_shapes=[
            pltpu.VMEM((local, cols, 2 * part, n), jnp.float32),
            pltpu.VMEM((2 * cols, n), jnp.float32),
        ],
        compiler_params=pltpu.CompilerParams(
            dimension_semantics=("arbitrary", "arbitrary"), vmem_limit_bytes=40 << 20
        ),
        cost_estimate=cost(local * rows * cols, (reach * local - reach * (reach + 1) // 2) * rows * cols, n),
        name="own_pairs",
    )(patches, *tabs)

    grid = {}
    for r in range(reach):
        count = reach - r
        own_specs = [
            pl.BlockSpec((1, 1, cols, 2 * part, n), functools.partial(lambda k, i: (k, i, 0, 0, 0), k))
            for k in range(r, reach)
        ]
        far = pl.pallas_call(
            functools.partial(far_kernel, count),
            grid=(rows,),
            in_specs=[pl.BlockSpec(patch_block, lambda i: (0, i, 0, 0, 0))] + tab_specs + own_specs,
            out_specs=pl.BlockSpec((count, 1, TILE, 2 * cols), lambda i: (0, i, 0, 0)),
            out_shape=jax.ShapeDtypeStruct((count, rows, TILE, 2 * cols), jnp.float32),
            scratch_shapes=[
                pltpu.VMEM((cols, 2 * part, n), jnp.float32),
                pltpu.VMEM((2 * cols, n), jnp.float32),
            ],
            compiler_params=pltpu.CompilerParams(
                dimension_semantics=("arbitrary",), vmem_limit_bytes=24 << 20
            ),
            cost_estimate=cost(rows * cols, count * rows * cols, n),
            name=f"far_pairs_{r}",
        )(ahead[r], *tabs, *([tail] * count))
        for item in range(count):
            section = local - reach + r + item
            grid[section, local + r - section] = far[item]
    stats = jnp.stack(
        [
            jnp.stack([grid.get((s, o), red[s, o - 1]) for o in range(1, reach + 1)], 0)
            for s in range(local)
        ],
        0,
    )

    placed = lax.axis_index("sec") * local + jnp.arange(local, dtype=jnp.int32)
    offsets = jnp.arange(1, reach + 1, dtype=jnp.int32)
    weights = pair_flags.astype(jnp.float32) * (
        placed[:, None] + offsets[None, :] < groups * local
    ).astype(jnp.float32)
    area = float(n * n)
    total = stats[..., 0, cols:] / area + EPSILON
    ratio = jnp.stack([stats[..., 0, :cols], stats[..., 1, cols:]], 0) / area / total
    measured = ratio * weights[None, :, :, None, None]

    span = rows * cols
    lanes = jnp.concatenate(
        [
            jnp.transpose(measured, (1, 0, 2, 3, 4)).reshape(local, 2, reach * span),
            jnp.transpose(nodes, (1, 0, 2, 3)).reshape(local, 2, span),
        ],
        axis=2,
    )
    lanes = jnp.pad(lanes, ((0, 0), (0, 0), (0, LANES // 2 - (reach + 1) * span)))
    flat = jnp.pad(weights.reshape(1, local * reach), ((0, 0), (0, LANES - local * reach)))
    base = jnp.concatenate([lanes.reshape(local, LANES), flat], axis=0)
    base = jnp.pad(base, ((0, TILE - local - 1), (0, 0)))

    sizes = (groups, tiles, local, reach, span, tiles * rows, cols)
    vmem = pl.BlockSpec(memory_space=pltpu.VMEM)
    moved = pl.pallas_call(
        functools.partial(relax_kernel, sizes),
        in_specs=[vmem],
        out_specs=vmem,
        out_shape=jax.ShapeDtypeStruct((TILE, LANES), jnp.float32),
        scratch_shapes=[
            pltpu.VMEM((groups * tiles, TILE, LANES), jnp.float32),
            pltpu.VMEM((reach + 1, groups * local, LANES), jnp.float32),
            pltpu.VMEM((reach, groups * local, LANES), jnp.float32),
            pltpu.SemaphoreType.DMA((groups * tiles,)),
            pltpu.SemaphoreType.DMA((groups * tiles,)),
        ],
        compiler_params=pltpu.CompilerParams(
            collective_id=0, has_side_effects=True, vmem_limit_bytes=24 << 20
        ),
        name="relax",
    )(base)
    positions = moved[:local].reshape(local, 2, LANES // 2)[:, :, :span]
    positions = jnp.transpose(positions.reshape(local, 2, rows, cols), (1, 0, 2, 3))
    return (positions, measured)


def solution(mesh):
    placed = (P("sec", "tile", None, None, None), P("sec", None), P(None, "sec", "tile", None))
    return jax.shard_map(
        shards,
        mesh=mesh,
        in_specs=placed,
        out_specs=(P(None, "sec", "tile", None), P(None, "sec", None, "tile", None)),
        check_vma=False,
    )
```

time: 269 us -> 68.9 us (0.26)
  other arithmetic: 62.7 us -> 1.87 us
  local copies, waits for them, and re-layouts: 61.5 us -> 7.17 us
  Pallas kernels: 0 us -> 54.1 us
  waiting for transfers between devices: 50 us -> 0.64 us
  starting transfers between devices: 48.8 us -> 3.86 us
  matrix products: 29.1 us -> 0 us
  blocking collectives: 11.7 us -> 0 us
    pallas_call x0 -> x5, Pallas kernels: none -> 54.1 us  [the longest x1 26.2 us: shards(): pl.pallas_call(functools.partial(own_kernel, reach), grid=(rows, local),...]
    ppermute x18 -> x3, waiting for transfers between devices: 50 us -> 0.64 us  [shards(): lax.ppermute(patches[r:r + 1], 'sec', back_by_one)]
    dynamic_slice x54 -> x0, local copies, waits for them, and re-layouts: 46.5 us -> none  [shards(): lax.map(one_section, (own, extended[step + 1:step + 1 + local], weights[:...]
    ppermute x18 -> x3, starting transfers between devices: 48.8 us -> 3.86 us  [shards(): lax.ppermute(patches[r:r + 1], 'sec', back_by_one)]
    convert_element_type x37 -> x0, other arithmetic: 31.5 us -> none  [the longest x18 31.4 us: measure(): right = second_spec.astype(jnp.float32)]
    dot_general x22 -> x0, matrix products: 29.1 us -> none  [the longest x18 18 us: measure(): jnp.einsum('arj,...rjk->...ak', tabs[3], back, preferred_element_type=jnp...]
    mul x29 -> x1, other arithmetic: 13.2 us -> 0.71 us  [shards(): measured = ratio * weights[None, :, :, None, None]]
    all_gather x2 -> x0, blocking collectives: 11.7 us -> none  [the longest x1 6.21 us: shards(): node_full = lax.all_gather(nodes, 'tile', axis=2, tiled=True)]
  transfers between devices with their start and end apart: 18 -> 3, of which waited for: 16 -> 1; matrix products, arithmetic and copies ran while one was open for 54% -> 3% of each run, Pallas kernels for 0% -> 50%
where the time goes in v1:
time: 68.9 us; the launch traced here: 68.5 us
  Pallas kernels  54.1 us (79%)
  local copies, waits for them, and re-layouts  7.17 us (10%)
  starting transfers between devices  3.86 us (6%)
  other arithmetic  1.87 us (3%)
  between operations  0.82 us (1%)
    pallas_call x1, Pallas kernels, shards(): pl.pallas_call(functools.partial(own_kernel, reach), grid=(rows, local),...  26.2 us
    pallas_call x1, Pallas kernels, shards(): pl.pallas_call(functools.partial(relax_kernel, sizes), in_specs=[vmem], o...  16.7 us
    pallas_call x3, Pallas kernels, shards(): pl.pallas_call(functools.partial(far_kernel, count), grid=(rows,), in_spe...  11.3 us
    ppermute x3, starting transfers between devices, shards(): lax.ppermute(patches[r:r + 1], 'sec', back_by_one)  3.86 us
    unnamed x13, local copies, waits for them, and re-layouts  3.12 us
    slice x1, local copies, waits for them, and re-layouts, shards(): patches[r:r + 1]  2.71 us
  transfers between devices with their start and end apart: 3, of which 1 were waited for; matrix products, arithmetic and copies ran while one was open for 3% of the time, Pallas kernels for 50%

profile of v1, /device:TPU:0, one launch (start us, length us, event | category | flops | bytes accessed | tf_op | source)
XLA Modules:
  0.0 68.5 jit_solution(16449598036608753926)
XLA Ops:
  0.6 0.0 copy-start.5
  0.6 0.0 copy-start.2
  0.7 0.0 copy-start
  0.7 2.7 %fusion.9 = (bf16[1,2,8,128,128]{4,3,2,1,0:T(8,128)(2,1)}, bf16[1,2,8,128,128]{4,3,2,1,0:T(8,128)(2,1)}, bf16[1,2,8,128,128]{4,3,2,1,0:T(8,128)(2,1)}) fusion(bf16[6,2,8,128,128]{4,3,2,1,0:T(8,128)(2,1)} %x.5), kind=kLoop, calls=%fused_computation.36 | loop fusion | bytes 3145728 | tf_op jit(solution)/shard_map/slice | solution.py:267
  3.4 1.3 %collective-permute-start.2 = (bf16[1,2,8,128,128]{4,3,2,1,0:T(8,128)(2,1)}, bf16[1,2,8,128,128]{4,3,2,1,0:T(8,128)(2,1)}, u32[]{:S(2)}, u32[]{:S(2)}) collective-permute-start(bf16[1,2,8,128,128]{4,3,2,1,0:T(8,128)(2,1)} %get-tuple-element.8), channel_id=1, source_target_pairs={{4,0},{8,4},{12,8},{16,12},{20,16},{24,20},{28,24},{5,1},{9,5},{13... | collective-permute-start | bytes 1572872 | tf_op jit(solution)/shard_map/ppermute | solution.py:267
  4.7 1.3 %collective-permute-start = (bf16[1,2,8,128,128]{4,3,2,1,0:T(8,128)(2,1)}, bf16[1,2,8,128,128]{4,3,2,1,0:T(8,128)(2,1)}, u32[]{:S(2)}, u32[]{:S(2)}) collective-permute-start(bf16[1,2,8,128,128]{4,3,2,1,0:T(8,128)(2,1)} %get-tuple-element.9), channel_id=1, source_target_pairs={{4,0},{8,4},{12,8},{16,12},{20,16},{24,20},{28,24},{5,1},{9,5},{13... | collective-permute-start | bytes 1572872 | tf_op jit(solution)/shard_map/ppermute | solution.py:267
  6.0 1.3 %collective-permute-start.1 = (bf16[1,2,8,128,128]{4,3,2,1,0:T(8,128)(2,1)}, bf16[1,2,8,128,128]{4,3,2,1,0:T(8,128)(2,1)}, u32[]{:S(2)}, u32[]{:S(2)}) collective-permute-start(bf16[1,2,8,128,128]{4,3,2,1,0:T(8,128)(2,1)} %get-tuple-element.10), channel_id=1, source_target_pairs={{4,0},{8,4},{12,8},{16,12},{20,16},{24,20},{28,24},{5,1},{9,5},{13... | collective-permute-start | bytes 1572872 | tf_op jit(solution)/shard_map/ppermute | solution.py:267
  7.3 0.8 %convert_select_fusion = f32[6,3]{0,1:T(4,128)S(1)} fusion(s32[6,3]{0,1:T(4,128)} %param.9, s32[3]{0:T(128)S(1)} %iota_add_fusion, s32[6]{0:T(128)S(1)} %iota_add_fusion.1), kind=kLoop, calls=%fused_computation.32 | loop fusion | flops 72 | bytes 180 | tf_op jit(solution)/shard_map/mul | solution.py:329
  8.0 0.1 copy.17
  8.1 0.1 reshape.44
  8.2 0.8 %reshape.48 = f32[6,2,16]{2,0,1:T(8,128)S(1)} reshape(f32[6,2,2,8]{3,2,0,1:T(2,128)} %bitcast.72) | data formatting | bytes 1536 | tf_op jit(solution)/shard_map/reshape | solution.py:341
  9.0 0.0 copy-done.5
  9.0 0.0 copy-done.2
  9.0 0.0 copy-done
  9.0 0.0 copy-start.1
  9.0 0.9 %copy-done.1 = bf16[256,256]{1,0:T(8,128)(2,1)S(1)} copy-done((bf16[256,256]{1,0:T(8,128)(2,1)S(1)}, bf16[256,256]{1,0:T(8,128)(2,1)}, u32[]{:S(2)}) %copy-start.1) | copy-done | bytes 131096
  9.9 0.0 copy-start.3
  9.9 0.8 %copy-done.3 = bf16[128,256]{1,0:T(8,128)(2,1)S(1)} copy-done((bf16[128,256]{1,0:T(8,128)(2,1)S(1)}, bf16[128,256]{1,0:T(8,128)(2,1)}, u32[]{:S(2)}) %copy-start.3) | copy-done | bytes 65560
  10.8 0.0 copy-start.4
  10.8 0.8 %copy-done.4 = bf16[128,128]{1,0:T(8,128)(2,1)S(1)} copy-done((bf16[128,128]{1,0:T(8,128)(2,1)S(1)}, bf16[128,128]{1,0:T(8,128)(2,1)}, u32[]{:S(2)}) %copy-start.4) | copy-done | bytes 32792
  11.5 26.2 %own_pairs.1 = (f32[6,3,2,8,16]{4,3,2,1,0:T(8,128)S(1)}, bf16[3,2,8,144,128]{4,3,2,1,0:T(8,128)(2,1)S(1)}) custom-call(bf16[6,2,8,128,128]{4,3,2,1,0:T(8,128)(2,1)S(1)} %copy-done, bf16[128,256]{1,0:T(8,128)(2,1)S(1)} %copy-done.3, bf16[144,256]{1,0:T(8,128)(2,1)S(1)} %copy-done.2, bf16[256,256]{1,0:T(8,128)(2,1)S(1)} %copy-done.1, ...), custom_call_target="tpu_custom_call" | custom-call | flops 14495514624 | bytes 25165824 | tf_op jit(solution)/shard_map/own_pairs/pallas_call | solution.py:270
  37.8 0.0 collective-permute-done.x
  37.8 4.5 %far_pairs_0.1 = f32[3,2,8,16]{3,2,1,0:T(8,128)S(1)} custom-call(bf16[1,2,8,128,128]{4,3,2,1,0:T(8,128)(2,1)} %collective-permute-done.x, bf16[128,256]{1,0:T(8,128)(2,1)S(1)} %copy-done.3, bf16[144,256]{1,0:T(8,128)(2,1)S(1)} %copy-done.2, bf16[256,256]{1,0:T(8,128)(2,1)S(1)} %copy-done.1, bf16[128,128]{1,0:T(8,128)(2,1)S(1)} %copy-done.4, ...), custom_call_target="tpu_custom_call" | custom-call | flops 3221225472 | bytes 4194304 | tf_op jit(solution)/shard_map/far_pairs_0/pallas_call | solution.py:300
  42.3 0.6 collective-permute-done.1.x
  43.0 3.8 %far_pairs_1.1 = f32[2,2,8,16]{3,2,1,0:T(8,128)S(1)} custom-call(bf16[1,2,8,128,128]{4,3,2,1,0:T(8,128)(2,1)} %collective-permute-done.1.x, bf16[128,256]{1,0:T(8,128)(2,1)S(1)} %copy-done.3, bf16[144,256]{1,0:T(8,128)(2,1)S(1)} %copy-done.2, bf16[256,256]{1,0:T(8,128)(2,1)S(1)} %copy-done.1, bf16[128,128]{1,0:T(8,128)(2,1)S(1)} %copy-done.4, ...), custom_call_target="tpu_custom_call" | custom-call | flops 2415919104 | bytes 4194304 | tf_op jit(solution)/shard_map/far_pairs_1/pallas_call | solution.py:300
  46.8 0.0 collective-permute-done.2.x
  46.8 3.0 %far_pairs_2.1 = f32[1,2,8,16]{3,2,1,0:T(8,128)S(1)} custom-call(bf16[1,2,8,128,128]{4,3,2,1,0:T(8,128)(2,1)} %collective-permute-done.2.x, bf16[128,256]{1,0:T(8,128)(2,1)S(1)} %copy-done.3, bf16[144,256]{1,0:T(8,128)(2,1)S(1)} %copy-done.2, bf16[256,256]{1,0:T(8,128)(2,1)S(1)} %copy-done.1, bf16[128,128]{1,0:T(8,128)(2,1)S(1)} %copy-done.4, ...), custom_call_target="tpu_custom_call" | custom-call | flops 1610612736 | bytes 4194304 | tf_op jit(solution)/shard_map/far_pairs_2/pallas_call | solution.py:300
  49.8 0.2 fusion.8
  50.0 0.1 fusion.12
  50.1 0.7 %fusion.1 = f32[2,6,3,2,8]{4,3,2,1,0:T(2,128)} fusion(f32[1,6,3,2,8]{4,3,2,1,0:T(2,128)S(1)} %bitcast.67, f32[1,6,3,2,8]{4,3,2,1,0:T(2,128)S(1)} %bitcast.69, f32[6,3]{1,0:T(8,128)S(1)} %copy.17, f32[6,3,2,8]{3,2,1,0:T(2,128)S(1)} %bitcast.65), kind=kLoop, calls=%fused_computation.2 | loop fusion | flops 2304 | bytes 5832 | tf_op jit(solution)/shard_map/mul | solution.py:335
  50.8 0.1 reshape.47
  50.9 0.1 pad_maximum_fusion
  51.0 0.1 reshape.43
  51.1 16.7 %relax.1 = f32[8,128]{1,0:T(8,128)S(1)} custom-call(f32[8,128]{1,0:T(8,128)S(1)} %pad.9.base), custom_call_target="tpu_custom_call" | custom-call | tf_op jit(solution)/shard_map/relax/pallas_call | solution.py:352
  67.7 0.1 reshape.45
  67.8 0.1 reshape.46
  67.9 0.6 copy.21
  (15 shorter events, 0.1 us)
Async XLA Ops:
  0.6 8.4 %copy-start.5 = (f32[8,128]{1,0:T(8,128)S(1)}, f32[8,128]{1,0:T(8,128)}, u32[]{:S(2)}) copy-start(f32[8,128]{1,0:T(8,128)} %constant.37.clone.weigh) | copy-start | bytes 12292
  0.6 8.4 %copy-start.2 = (bf16[144,256]{1,0:T(8,128)(2,1)S(1)}, bf16[144,256]{1,0:T(8,128)(2,1)}, u32[]{:S(2)}) copy-start(bf16[144,256]{1,0:T(8,128)(2,1)} %constant.34.clone.second) | copy-start | bytes 221188
  0.7 8.4 %copy-start = (bf16[6,2,8,128,128]{4,3,2,1,0:T(8,128)(2,1)S(1)}, bf16[6,2,8,128,128]{4,3,2,1,0:T(8,128)(2,1)}, u32[]{:S(2)}) copy-start(bf16[6,2,8,128,128]{4,3,2,1,0:T(8,128)(2,1)} %x.5) | copy-start | bytes 9437188
  3.4 43.4 %collective-permute-start.2 = (bf16[1,2,8,128,128]{4,3,2,1,0:T(8,128)(2,1)}, bf16[1,2,8,128,128]{4,3,2,1,0:T(8,128)(2,1)}, u32[]{:S(2)}, u32[]{:S(2)}) collective-permute-start(bf16[1,2,8,128,128]{4,3,2,1,0:T(8,128)(2,1)} %get-tuple-element.8), channel_id=1, source_target_pairs={{4,0},{8,4},{12,8},{16,12},{20,16},{24,20},{28,24},{5,1},{9,5},{13... | collective-permute-start | bytes 1572872 | tf_op jit(solution)/shard_map/ppermute | solution.py:267
  4.7 33.2 %collective-permute-start = (bf16[1,2,8,128,128]{4,3,2,1,0:T(8,128)(2,1)}, bf16[1,2,8,128,128]{4,3,2,1,0:T(8,128)(2,1)}, u32[]{:S(2)}, u32[]{:S(2)}) collective-permute-start(bf16[1,2,8,128,128]{4,3,2,1,0:T(8,128)(2,1)} %get-tuple-element.9), channel_id=1, source_target_pairs={{4,0},{8,4},{12,8},{16,12},{20,16},{24,20},{28,24},{5,1},{9,5},{13... | collective-permute-start | bytes 1572872 | tf_op jit(solution)/shard_map/ppermute | solution.py:267
  6.0 37.0 %collective-permute-start.1 = (bf16[1,2,8,128,128]{4,3,2,1,0:T(8,128)(2,1)}, bf16[1,2,8,128,128]{4,3,2,1,0:T(8,128)(2,1)}, u32[]{:S(2)}, u32[]{:S(2)}) collective-permute-start(bf16[1,2,8,128,128]{4,3,2,1,0:T(8,128)(2,1)} %get-tuple-element.10), channel_id=1, source_target_pairs={{4,0},{8,4},{12,8},{16,12},{20,16},{24,20},{28,24},{5,1},{9,5},{13... | collective-permute-start | bytes 1572872 | tf_op jit(solution)/shard_map/ppermute | solution.py:267
  9.0 0.9 %copy-start.1 = (bf16[256,256]{1,0:T(8,128)(2,1)S(1)}, bf16[256,256]{1,0:T(8,128)(2,1)}, u32[]{:S(2)}) copy-start(bf16[256,256]{1,0:T(8,128)(2,1)} %constant.35.clone.inverse) | copy-start | bytes 393220
  9.9 0.8 %copy-start.3 = (bf16[128,256]{1,0:T(8,128)(2,1)S(1)}, bf16[128,256]{1,0:T(8,128)(2,1)}, u32[]{:S(2)}) copy-start(bf16[128,256]{1,0:T(8,128)(2,1)} %constant.33.clone.first) | copy-start | bytes 196612
  10.8 0.8 %copy-start.4 = (bf16[128,128]{1,0:T(8,128)(2,1)S(1)}, bf16[128,128]{1,0:T(8,128)(2,1)}, u32[]{:S(2)}) copy-start(bf16[128,128]{1,0:T(8,128)(2,1)} %constant.36.clone.last) | copy-start | bytes 98308

commit v2 on v1

--- a/solution.py
+++ b/solution.py
@@ -115,11 +115,11 @@
     def put(c, value):
         spec[step, c] = value
 
-        @pl.when(step >= local - reach)
-        def _():
-            tail[jnp.maximum(step - (local - reach), 0), 0, c] = value.astype(tail.dtype)
-
     spectra(x[0, 0], first[...], second[...], put)
+
+    @pl.when(step >= local - reach)
+    def _():
+        tail[jnp.maximum(step - (local - reach), 0), 0] = spec[step].astype(tail.dtype)
 
     def body(offset, carry):
         red[step - offset, offset - 1, row] = pairs(

time: 68.9 us -> 64.2 us (0.932)
  Pallas kernels: 54.1 us -> 44.6 us
  waiting for transfers between devices: 0.64 us -> 5.42 us
    ppermute x3, waiting for transfers between devices: 0.64 us -> 5.42 us  [shards(): lax.ppermute(patches[r:r + 1], 'sec', back_by_one)]
    pallas_call x1, Pallas kernels: 26.2 us -> 21.4 us  [shards(): pl.pallas_call(functools.partial(own_kernel, reach), grid=(rows, local),...]
    pallas_call x1, Pallas kernels: 16.7 us -> 11.9 us  [shards(): pl.pallas_call(functools.partial(relax_kernel, sizes), in_specs=[vmem], o...]
  transfers between devices with their start and end apart: 3 -> 3, of which waited for: 1 -> 1; matrix products, arithmetic and copies ran while one was open for 3% -> 3% of each run, Pallas kernels for 50% -> 47%
where the time goes in v2:
time: 64.2 us; the launch traced here: 63.7 us
  Pallas kernels  44.6 us (69%)
  local copies, waits for them, and re-layouts  7.17 us (11%)
  waiting for transfers between devices  5.42 us (8%)
  starting transfers between devices  3.86 us (6%)
  other arithmetic  1.87 us (3%)
  between operations  0.82 us (1%)
    pallas_call x1, Pallas kernels, shards(): pl.pallas_call(functools.partial(own_kernel, reach), grid=(rows, local),...  21.4 us
    pallas_call x1, Pallas kernels, shards(): pl.pallas_call(functools.partial(relax_kernel, sizes), in_specs=[vmem], o...  11.9 us
    pallas_call x3, Pallas kernels, shards(): pl.pallas_call(functools.partial(far_kernel, count), grid=(rows,), in_spe...  11.3 us
    ppermute x3, waiting for transfers between devices, shards(): lax.ppermute(patches[r:r + 1], 'sec', back_by_one)  5.42 us
    ppermute x3, starting transfers between devices, shards(): lax.ppermute(patches[r:r + 1], 'sec', back_by_one)  3.86 us
    unnamed x13, local copies, waits for them, and re-layouts  3.12 us
    slice x1, local copies, waits for them, and re-layouts, shards(): patches[r:r + 1]  2.71 us
  transfers between devices with their start and end apart: 3, of which 1 were waited for; matrix products, arithmetic and copies ran while one was open for 3% of the time, Pallas kernels for 47%

profile of v2, /device:TPU:0, one launch (start us, length us, event | category | flops | bytes accessed | tf_op | source)
XLA Modules:
  0.0 63.7 jit_solution(2355212586675936870)
XLA Ops:
  0.6 0.0 copy-start.5
  0.6 0.0 copy-start.2
  0.7 0.0 copy-start
  0.7 2.7 %fusion.9 = (bf16[1,2,8,128,128]{4,3,2,1,0:T(8,128)(2,1)}, bf16[1,2,8,128,128]{4,3,2,1,0:T(8,128)(2,1)}, bf16[1,2,8,128,128]{4,3,2,1,0:T(8,128)(2,1)}) fusion(bf16[6,2,8,128,128]{4,3,2,1,0:T(8,128)(2,1)} %x.5), kind=kLoop, calls=%fused_computation.36 | loop fusion | bytes 3145728 | tf_op jit(solution)/shard_map/slice | solution.py:267
  3.4 1.3 %collective-permute-start.2 = (bf16[1,2,8,128,128]{4,3,2,1,0:T(8,128)(2,1)}, bf16[1,2,8,128,128]{4,3,2,1,0:T(8,128)(2,1)}, u32[]{:S(2)}, u32[]{:S(2)}) collective-permute-start(bf16[1,2,8,128,128]{4,3,2,1,0:T(8,128)(2,1)} %get-tuple-element.8), channel_id=1, source_target_pairs={{4,0},{8,4},{12,8},{16,12},{20,16},{24,20},{28,24},{5,1},{9,5},{13... | collective-permute-start | bytes 1572872 | tf_op jit(solution)/shard_map/ppermute | solution.py:267
  4.7 1.3 %collective-permute-start = (bf16[1,2,8,128,128]{4,3,2,1,0:T(8,128)(2,1)}, bf16[1,2,8,128,128]{4,3,2,1,0:T(8,128)(2,1)}, u32[]{:S(2)}, u32[]{:S(2)}) collective-permute-start(bf16[1,2,8,128,128]{4,3,2,1,0:T(8,128)(2,1)} %get-tuple-element.9), channel_id=1, source_target_pairs={{4,0},{8,4},{12,8},{16,12},{20,16},{24,20},{28,24},{5,1},{9,5},{13... | collective-permute-start | bytes 1572872 | tf_op jit(solution)/shard_map/ppermute | solution.py:267
  6.0 1.3 %collective-permute-start.1 = (bf16[1,2,8,128,128]{4,3,2,1,0:T(8,128)(2,1)}, bf16[1,2,8,128,128]{4,3,2,1,0:T(8,128)(2,1)}, u32[]{:S(2)}, u32[]{:S(2)}) collective-permute-start(bf16[1,2,8,128,128]{4,3,2,1,0:T(8,128)(2,1)} %get-tuple-element.10), channel_id=1, source_target_pairs={{4,0},{8,4},{12,8},{16,12},{20,16},{24,20},{28,24},{5,1},{9,5},{13... | collective-permute-start | bytes 1572872 | tf_op jit(solution)/shard_map/ppermute | solution.py:267
  7.3 0.8 %convert_select_fusion = f32[6,3]{0,1:T(4,128)S(1)} fusion(s32[6,3]{0,1:T(4,128)} %param.9, s32[3]{0:T(128)S(1)} %iota_add_fusion, s32[6]{0:T(128)S(1)} %iota_add_fusion.1), kind=kLoop, calls=%fused_computation.32 | loop fusion | flops 72 | bytes 180 | tf_op jit(solution)/shard_map/mul | solution.py:329
  8.0 0.1 copy.17
  8.1 0.1 reshape.44
  8.2 0.8 %reshape.48 = f32[6,2,16]{2,0,1:T(8,128)S(1)} reshape(f32[6,2,2,8]{3,2,0,1:T(2,128)} %bitcast.72) | data formatting | bytes 1536 | tf_op jit(solution)/shard_map/reshape | solution.py:341
  9.0 0.0 copy-done.5
  9.0 0.0 copy-done.2
  9.0 0.0 copy-done
  9.0 0.0 copy-start.1
  9.0 0.9 %copy-done.1 = bf16[256,256]{1,0:T(8,128)(2,1)S(1)} copy-done((bf16[256,256]{1,0:T(8,128)(2,1)S(1)}, bf16[256,256]{1,0:T(8,128)(2,1)}, u32[]{:S(2)}) %copy-start.1) | copy-done | bytes 131096
  9.9 0.0 copy-start.3
  9.9 0.8 %copy-done.3 = bf16[128,256]{1,0:T(8,128)(2,1)S(1)} copy-done((bf16[128,256]{1,0:T(8,128)(2,1)S(1)}, bf16[128,256]{1,0:T(8,128)(2,1)}, u32[]{:S(2)}) %copy-start.3) | copy-done | bytes 65560
  10.8 0.0 copy-start.4
  10.8 0.8 %copy-done.4 = bf16[128,128]{1,0:T(8,128)(2,1)S(1)} copy-done((bf16[128,128]{1,0:T(8,128)(2,1)S(1)}, bf16[128,128]{1,0:T(8,128)(2,1)}, u32[]{:S(2)}) %copy-start.4) | copy-done | bytes 32792
  11.5 21.4 %own_pairs.1 = (f32[6,3,2,8,16]{4,3,2,1,0:T(8,128)S(1)}, bf16[3,2,8,144,128]{4,3,2,1,0:T(8,128)(2,1)S(1)}) custom-call(bf16[6,2,8,128,128]{4,3,2,1,0:T(8,128)(2,1)S(1)} %copy-done, bf16[128,256]{1,0:T(8,128)(2,1)S(1)} %copy-done.3, bf16[144,256]{1,0:T(8,128)(2,1)S(1)} %copy-done.2, bf16[256,256]{1,0:T(8,128)(2,1)S(1)} %copy-done.1, ...), custom_call_target="tpu_custom_call" | custom-call | flops 14495514624 | bytes 25165824 | tf_op jit(solution)/shard_map/own_pairs/pallas_call | solution.py:270
  33.1 0.0 collective-permute-done.x
  33.1 4.5 %far_pairs_0.1 = f32[3,2,8,16]{3,2,1,0:T(8,128)S(1)} custom-call(bf16[1,2,8,128,128]{4,3,2,1,0:T(8,128)(2,1)} %collective-permute-done.x, bf16[128,256]{1,0:T(8,128)(2,1)S(1)} %copy-done.3, bf16[144,256]{1,0:T(8,128)(2,1)S(1)} %copy-done.2, bf16[256,256]{1,0:T(8,128)(2,1)S(1)} %copy-done.1, bf16[128,128]{1,0:T(8,128)(2,1)S(1)} %copy-done.4, ...), custom_call_target="tpu_custom_call" | custom-call | flops 3221225472 | bytes 4194304 | tf_op jit(solution)/shard_map/far_pairs_0/pallas_call | solution.py:300
  37.5 5.4 %collective-permute-done.1.x = bf16[1,2,8,128,128]{4,3,2,1,0:T(8,128)(2,1)} collective-permute-done((bf16[1,2,8,128,128]{4,3,2,1,0:T(8,128)(2,1)}, bf16[1,2,8,128,128]{4,3,2,1,0:T(8,128)(2,1)}, u32[]{:S(2)}, u32[]{:S(2)}) %collective-permute-start.1) | collective-permute-done | bytes 524320 | tf_op jit(solution)/shard_map/ppermute | solution.py:267
  43.0 3.8 %far_pairs_1.1 = f32[2,2,8,16]{3,2,1,0:T(8,128)S(1)} custom-call(bf16[1,2,8,128,128]{4,3,2,1,0:T(8,128)(2,1)} %collective-permute-done.1.x, bf16[128,256]{1,0:T(8,128)(2,1)S(1)} %copy-done.3, bf16[144,256]{1,0:T(8,128)(2,1)S(1)} %copy-done.2, bf16[256,256]{1,0:T(8,128)(2,1)S(1)} %copy-done.1, bf16[128,128]{1,0:T(8,128)(2,1)S(1)} %copy-done.4, ...), custom_call_target="tpu_custom_call" | custom-call | flops 2415919104 | bytes 4194304 | tf_op jit(solution)/shard_map/far_pairs_1/pallas_call | solution.py:300
  46.8 0.0 collective-permute-done.2.x
  46.8 3.0 %far_pairs_2.1 = f32[1,2,8,16]{3,2,1,0:T(8,128)S(1)} custom-call(bf16[1,2,8,128,128]{4,3,2,1,0:T(8,128)(2,1)} %collective-permute-done.2.x, bf16[128,256]{1,0:T(8,128)(2,1)S(1)} %copy-done.3, bf16[144,256]{1,0:T(8,128)(2,1)S(1)} %copy-done.2, bf16[256,256]{1,0:T(8,128)(2,1)S(1)} %copy-done.1, bf16[128,128]{1,0:T(8,128)(2,1)S(1)} %copy-done.4, ...), custom_call_target="tpu_custom_call" | custom-call | flops 1610612736 | bytes 4194304 | tf_op jit(solution)/shard_map/far_pairs_2/pallas_call | solution.py:300
  49.8 0.2 fusion.8
  50.0 0.1 fusion.12
  50.1 0.7 %fusion.1 = f32[2,6,3,2,8]{4,3,2,1,0:T(2,128)} fusion(f32[1,6,3,2,8]{4,3,2,1,0:T(2,128)S(1)} %bitcast.67, f32[1,6,3,2,8]{4,3,2,1,0:T(2,128)S(1)} %bitcast.69, f32[6,3]{1,0:T(8,128)S(1)} %copy.17, f32[6,3,2,8]{3,2,1,0:T(2,128)S(1)} %bitcast.65), kind=kLoop, calls=%fused_computation.2 | loop fusion | flops 2304 | bytes 5832 | tf_op jit(solution)/shard_map/mul | solution.py:335
  50.8 0.1 reshape.47
  50.9 0.1 pad_maximum_fusion
  51.0 0.1 reshape.43
  51.1 11.9 %relax.1 = f32[8,128]{1,0:T(8,128)S(1)} custom-call(f32[8,128]{1,0:T(8,128)S(1)} %pad.9.base), custom_call_target="tpu_custom_call" | custom-call | tf_op jit(solution)/shard_map/relax/pallas_call | solution.py:352
  62.9 0.1 reshape.45
  63.0 0.1 reshape.46
  63.1 0.6 copy.21
  (15 shorter events, 0.1 us)
Async XLA Ops:
  0.6 8.4 %copy-start.5 = (f32[8,128]{1,0:T(8,128)S(1)}, f32[8,128]{1,0:T(8,128)}, u32[]{:S(2)}) copy-start(f32[8,128]{1,0:T(8,128)} %constant.37.clone.weigh) | copy-start | bytes 12292
  0.6 8.4 %copy-start.2 = (bf16[144,256]{1,0:T(8,128)(2,1)S(1)}, bf16[144,256]{1,0:T(8,128)(2,1)}, u32[]{:S(2)}) copy-start(bf16[144,256]{1,0:T(8,128)(2,1)} %constant.34.clone.second) | copy-start | bytes 221188
  0.7 8.4 %copy-start = (bf16[6,2,8,128,128]{4,3,2,1,0:T(8,128)(2,1)S(1)}, bf16[6,2,8,128,128]{4,3,2,1,0:T(8,128)(2,1)}, u32[]{:S(2)}) copy-start(bf16[6,2,8,128,128]{4,3,2,1,0:T(8,128)(2,1)} %x.5) | copy-start | bytes 9437188
  3.4 43.4 %collective-permute-start.2 = (bf16[1,2,8,128,128]{4,3,2,1,0:T(8,128)(2,1)}, bf16[1,2,8,128,128]{4,3,2,1,0:T(8,128)(2,1)}, u32[]{:S(2)}, u32[]{:S(2)}) collective-permute-start(bf16[1,2,8,128,128]{4,3,2,1,0:T(8,128)(2,1)} %get-tuple-element.8), channel_id=1, source_target_pairs={{4,0},{8,4},{12,8},{16,12},{20,16},{24,20},{28,24},{5,1},{9,5},{13... | collective-permute-start | bytes 1572872 | tf_op jit(solution)/shard_map/ppermute | solution.py:267
  4.7 28.4 %collective-permute-start = (bf16[1,2,8,128,128]{4,3,2,1,0:T(8,128)(2,1)}, bf16[1,2,8,128,128]{4,3,2,1,0:T(8,128)(2,1)}, u32[]{:S(2)}, u32[]{:S(2)}) collective-permute-start(bf16[1,2,8,128,128]{4,3,2,1,0:T(8,128)(2,1)} %get-tuple-element.9), channel_id=1, source_target_pairs={{4,0},{8,4},{12,8},{16,12},{20,16},{24,20},{28,24},{5,1},{9,5},{13... | collective-permute-start | bytes 1572872 | tf_op jit(solution)/shard_map/ppermute | solution.py:267
  6.0 37.0 %collective-permute-start.1 = (bf16[1,2,8,128,128]{4,3,2,1,0:T(8,128)(2,1)}, bf16[1,2,8,128,128]{4,3,2,1,0:T(8,128)(2,1)}, u32[]{:S(2)}, u32[]{:S(2)}) collective-permute-start(bf16[1,2,8,128,128]{4,3,2,1,0:T(8,128)(2,1)} %get-tuple-element.10), channel_id=1, source_target_pairs={{4,0},{8,4},{12,8},{16,12},{20,16},{24,20},{28,24},{5,1},{9,5},{13... | collective-permute-start | bytes 1572872 | tf_op jit(solution)/shard_map/ppermute | solution.py:267
  9.0 0.9 %copy-start.1 = (bf16[256,256]{1,0:T(8,128)(2,1)S(1)}, bf16[256,256]{1,0:T(8,128)(2,1)}, u32[]{:S(2)}) copy-start(bf16[256,256]{1,0:T(8,128)(2,1)} %constant.35.clone.inverse) | copy-start | bytes 393220
  9.9 0.8 %copy-start.3 = (bf16[128,256]{1,0:T(8,128)(2,1)S(1)}, bf16[128,256]{1,0:T(8,128)(2,1)}, u32[]{:S(2)}) copy-start(bf16[128,256]{1,0:T(8,128)(2,1)} %constant.33.clone.first) | copy-start | bytes 196612
  10.8 0.8 %copy-start.4 = (bf16[128,128]{1,0:T(8,128)(2,1)S(1)}, bf16[128,128]{1,0:T(8,128)(2,1)}, u32[]{:S(2)}) copy-start(bf16[128,128]{1,0:T(8,128)(2,1)} %constant.36.clone.last) | copy-start | bytes 98308

commit v3 on v2

--- a/solution.py
+++ b/solution.py
@@ -9,6 +9,7 @@
 from jax.experimental.pallas import tpu as pltpu
 from jax.sharding import PartitionSpec as P
 
+
 SWEEPS = 8
 STEP_SIZE = 0.08
 EPSILON = 1e-06
@@ -23,42 +24,51 @@
     phase = (k[:, None] * k[None, :] % n) * (2.0 * math.pi / n)
     c = np.asarray(np.cos(phase), np.float32).astype(jnp.bfloat16).astype(np.float32)
     s = np.asarray(np.sin(phase), np.float32).astype(jnp.bfloat16).astype(np.float32)
-    first = np.concatenate([c, s], 1)
     part = h + TILE
-    second = np.zeros((2 * part, 2 * n), np.float32)
-    second[: h + 1, :n] = c[: h + 1]
-    second[: h + 1, n:] = -s[: h + 1]
-    second[part : part + h + 1, :n] = -s[: h + 1]
-    second[part : part + h + 1, n:] = -c[: h + 1]
+    first = np.zeros((2 * part, 2 * n), np.float32)
+    first[: h + 1, :n] = c[: h + 1]
+    first[part : part + h, :n] = s[:h]
+    second = np.concatenate([np.concatenate([c, -s], 1), np.concatenate([-s, -c], 1)], 0)
     inverse = np.concatenate([np.concatenate([c, s], 1), np.concatenate([-s, c], 1)], 0)
     order = (np.arange(n) - h) % n
-    last = np.zeros((n, n), np.float32)
+    last = np.zeros((n, 2 * n), np.float32)
     last[:, 0] = c[order, 0]
     last[:, 1:h] = 2.0 * c[order, 1:h]
     last[:, h] = c[order, h]
-    last[:, h + 1 :] = -2.0 * s[order, 1:h]
+    last[:, h + 1 : n] = -2.0 * s[order, 1:h]
     last *= 1.0 / float(n) ** 3
-    weigh = np.zeros((TILE, n), np.float32)
-    weigh[0] = 1.0
-    weigh[1] = np.where(k < h, k, k - n)
-    low = lambda a: np.asarray(a).astype(jnp.bfloat16)
-    return low(first), low(second), low(inverse), low(last), weigh
+    return np.concatenate([first, second, inverse, last], 0).astype(jnp.bfloat16)
+
+
+def open_tables(tab, n):
+    part = n // 2 + TILE
+    first = tab[: 2 * part, :n]
+    second = tab[2 * part : 2 * part + 2 * n]
+    inverse = tab[2 * part + 2 * n : 2 * part + 4 * n]
+    last = tab[2 * part + 4 * n :, :n]
+    sub = lax.broadcasted_iota(jnp.int32, (TILE, n), 0)
+    lane = lax.broadcasted_iota(jnp.int32, (TILE, n), 1)
+    shift = jnp.where(lane < n // 2, lane, lane - n).astype(jnp.float32)
+    weigh = jnp.where(sub == 0, 1.0, jnp.where(sub == 1, shift, 0.0))
+    return (first, second), (inverse, last, weigh)
 
 
 def spectra(x, first, second, put):
     cols, n = x.shape[0], x.shape[-1]
-    half = jnp.dot(x.reshape(cols * n, n), first, preferred_element_type=jnp.float32)
-    half = half.astype(jnp.bfloat16)
+    part = n // 2 + TILE
+    lines = []
     for c in range(0, cols, 2):
-        sides = []
-        for d in (c, c + 1):
-            mine = half[d * n : (d + 1) * n]
-            sides.append(jnp.concatenate([mine[:, :n], mine[:, n:]], axis=0))
-        spec = jnp.dot(
-            second, jnp.concatenate(sides, axis=1), preferred_element_type=jnp.float32
-        )
-        put(c, spec[:, :n])
-        put(c + 1, spec[:, n:])
+        y = jnp.dot(
+            first, jnp.concatenate([x[c], x[c + 1]], axis=1), preferred_element_type=jnp.float32
+        )
+        for d in (0, 1):
+            mine = y[:, d * n : (d + 1) * n]
+            lines.append(jnp.concatenate([mine[:part], mine[part:]], axis=1))
+    lines = jnp.concatenate(lines, axis=0).astype(jnp.bfloat16)
+    spec = jnp.dot(lines, second, preferred_element_type=jnp.float32)
+    for c in range(cols):
+        mine = spec[c * part : (c + 1) * part]
+        put(c, mine[:, :n], mine[:, n:])
 
 
 def pairs(get_a, get_b, cols, n, inverse, last, weigh, sums):
@@ -106,16 +116,20 @@
     )
 
 
-def own_kernel(reach, x, first, second, inverse, last, weigh, red, tail, spec, sums):
+def own_kernel(reach, x, tab, red, tail, spec, sums):
     row = pl.program_id(0)
     step = pl.program_id(1)
     local = pl.num_programs(1)
     cols, n = x.shape[2], x.shape[-1]
 
-    def put(c, value):
-        spec[step, c] = value
-
-    spectra(x[0, 0], first[...], second[...], put)
+    part = n // 2 + TILE
+    forward, inverse = open_tables(tab, n)
+
+    def put(c, real, imag):
+        spec[step, c, :part] = real
+        spec[step, c, part:] = imag
+
+    spectra(x.at[0, 0], *forward, put)
 
     @pl.when(step >= local - reach)
     def _():
@@ -125,26 +139,30 @@
         red[step - offset, offset - 1, row] = pairs(
             lambda c: spec[step - offset, c],
             lambda c: spec[step, c],
-            cols, n, inverse[...], last[...], weigh[...], sums,
+            cols, n, *inverse, sums,
         )
         return carry
 
     lax.fori_loop(1, jnp.minimum(step, reach) + 1, body, 0)
 
 
-def far_kernel(count, x, first, second, inverse, last, weigh, *rest):
+def far_kernel(count, x, tab, *rest):
     own, red, spec, sums = rest[:count], rest[count], rest[count + 1], rest[count + 2]
     cols, n = x.shape[2], x.shape[-1]
 
-    def put(c, value):
-        spec[c] = value
-
-    spectra(x[0, 0], first[...], second[...], put)
+    part = n // 2 + TILE
+    forward, inverse = open_tables(tab, n)
+
+    def put(c, real, imag):
+        spec[c, :part] = real
+        spec[c, part:] = imag
+
+    spectra(x.at[0, 0], *forward, put)
     for item in range(count):
         red[item, 0] = pairs(
             lambda c: own[item][0, 0, c].astype(jnp.float32),
             lambda c: spec[c],
-            cols, n, inverse[...], last[...], weigh[...], sums,
+            cols, n, *inverse, sums,
         )
 
 
@@ -168,6 +186,7 @@
     tile = lax.axis_index("tile")
     me = sec * tiles + tile
     count = groups * tiles
+    unroll = count <= 64
 
     def place(index):
         return (index // tiles, index % tiles)
@@ -180,7 +199,7 @@
         )
         return carry
 
-    lax.fori_loop(1, count, greet, 0)
+    lax.fori_loop(1, count, greet, 0, unroll=unroll)
     pl.semaphore_wait(barrier, count - 1)
 
     def copy(slot, peer):
@@ -197,7 +216,7 @@
         copy(me, (me + d) % count).start()
         return carry
 
-    lax.fori_loop(1, count, start, 0)
+    lax.fori_loop(1, count, start, 0, unroll=unroll)
     slots[me] = base[...]
 
     def finish(d, carry):
@@ -206,7 +225,7 @@
         copy(me, peer).wait_send()
         return carry
 
-    lax.fori_loop(1, count, finish, 0)
+    lax.fori_loop(1, count, finish, 0, unroll=unroll)
 
     lane = lax.broadcasted_iota(jnp.int32, (TILE, LANES), 1)
     sub = lax.broadcasted_iota(jnp.int32, (TILE, LANES), 0)
@@ -261,16 +280,18 @@
     reach = pair_flags.shape[1]
     groups, tiles = lax.axis_size("sec"), lax.axis_size("tile")
     part = n // 2 + TILE
-    tabs = [jnp.asarray(t) for t in tables(n)]
-    tab_specs = [fixed(t) for t in tabs]
+    tab = jnp.asarray(tables(n))
     back_by_one = [(i, i - 1) for i in range(1, groups)]
-    ahead = [lax.ppermute(patches[r : r + 1], "sec", back_by_one) for r in range(reach)]
+    head = patches[: reach - 1]
+    early = lax.ppermute(head, "sec", back_by_one)
+    _, rest = lax.optimization_barrier((head, patches))
+    late = lax.ppermute(rest[reach - 1 : reach], "sec", back_by_one)
 
     patch_block = (1, 1, cols, n, n)
     red, tail = pl.pallas_call(
         functools.partial(own_kernel, reach),
         grid=(rows, local),
-        in_specs=[pl.BlockSpec(patch_block, lambda i, s: (s, i, 0, 0, 0))] + tab_specs,
+        in_specs=[pl.BlockSpec(patch_block, lambda i, s: (s, i, 0, 0, 0))] + [fixed(tab)],
         out_specs=[
             pl.BlockSpec((local, reach, rows, TILE, 2 * cols), lambda i, s: (0, 0, 0, 0, 0)),
             pl.BlockSpec((reach, 1, cols, 2 * part, n), lambda i, s: (0, i, 0, 0, 0)),
@@ -288,19 +309,20 @@
         ),
         cost_estimate=cost(local * rows * cols, (reach * local - reach * (reach + 1) // 2) * rows * cols, n),
         name="own_pairs",
-    )(patches, *tabs)
+    )(patches, tab)
 
     grid = {}
     for r in range(reach):
         count = reach - r
+        received, spot = (early, r) if r < reach - 1 else (late, 0)
         own_specs = [
             pl.BlockSpec((1, 1, cols, 2 * part, n), functools.partial(lambda k, i: (k, i, 0, 0, 0), k))
             for k in range(r, reach)
         ]
-        far = pl.pallas_call(
+        far_call = pl.pallas_call(
             functools.partial(far_kernel, count),
             grid=(rows,),
-            in_specs=[pl.BlockSpec(patch_block, lambda i: (0, i, 0, 0, 0))] + tab_specs + own_specs,
+            in_specs=[pl.BlockSpec(patch_block, functools.partial(lambda k, i: (k, i, 0, 0, 0), spot))] + [fixed(tab)] + own_specs,
             out_specs=pl.BlockSpec((count, 1, TILE, 2 * cols), lambda i: (0, i, 0, 0)),
             out_shape=jax.ShapeDtypeStruct((count, rows, TILE, 2 * cols), jnp.float32),
             scratch_shapes=[
@@ -311,8 +333,8 @@
                 dimension_semantics=("arbitrary",), vmem_limit_bytes=24 << 20
             ),
             cost_estimate=cost(rows * cols, count * rows * cols, n),
-            name=f"far_pairs_{r}",
-        )(ahead[r], *tabs, *([tail] * count))
+        )
+        far = far_call(received, tab, *([tail] * count))
         for item in range(count):
             section = local - reach + r + item
             grid[section, local + r - section] = far[item]

time: 64.2 us -> 68.6 us (1.069)
  waiting for transfers between devices: 5.42 us -> 12.8 us
  Pallas kernels: 44.6 us -> 40.7 us
  local copies, waits for them, and re-layouts: 7.17 us -> 10.3 us
  starting transfers between devices: 3.86 us -> 2.56 us
  other arithmetic: 1.87 us -> 1.17 us
    ppermute x3 -> x2, waiting for transfers between devices: 5.42 us -> 12.8 us  [the longest x1 12.8 us: shards(): late = lax.ppermute(rest[reach - 1:reach], 'sec', back_by_one)]
    unnamed x13 -> x15, local copies, waits for them, and re-layouts: 3.12 us -> 5.3 us
    pallas_call x1, Pallas kernels: 21.4 us -> 19.7 us  [shards(): pl.pallas_call(functools.partial(own_kernel, reach), grid=(rows, local),...]
    slice x1 -> x2, local copies, waits for them, and re-layouts: 2.71 us -> 4.36 us  [the longest x1 2.47 us: shards(): head = patches[:reach - 1]]
    ppermute x3 -> x2, starting transfers between devices: 3.86 us -> 2.56 us  [the longest x1 1.28 us: shards(): early = lax.ppermute(head, 'sec', back_by_one)]
    pallas_call x1, Pallas kernels: 11.9 us -> 10.7 us  [shards(): pl.pallas_call(functools.partial(relax_kernel, sizes), in_specs=[vmem], o...]
    pallas_call x3, Pallas kernels: 11.3 us -> 10.3 us  [shards(): far = far_call(received, tab, *[tail] * count)]
    reshape x2, local copies, waits for them, and re-layouts: 0.79 us -> 0.09 us  [shards(): jnp.transpose(nodes, (1, 0, 2, 3)).reshape(local, 2, span)]
  transfers between devices with their start and end apart: 3 -> 2, of which waited for: 1 -> 1; matrix products, arithmetic and copies ran while one was open for 3% -> 3% of each run, Pallas kernels for 47% -> 33%
where the time goes in v3:
time: 68.6 us; the launch traced here: 68.3 us
  Pallas kernels  40.7 us (59%)
  waiting for transfers between devices  12.8 us (19%)
  local copies, waits for them, and re-layouts  10.3 us (15%)
  starting transfers between devices  2.56 us (4%)
  other arithmetic  1.17 us (2%)
  between operations  0.78 us (1%)
    pallas_call x1, Pallas kernels, shards(): pl.pallas_call(functools.partial(own_kernel, reach), grid=(rows, local),...  19.7 us
    ppermute x1, waiting for transfers between devices, shards(): late = lax.ppermute(rest[reach - 1:reach], 'sec', back_by_one)  12.8 us
    pallas_call x1, Pallas kernels, shards(): pl.pallas_call(functools.partial(relax_kernel, sizes), in_specs=[vmem], o...  10.7 us
    pallas_call x3, Pallas kernels, shards(): far = far_call(received, tab, *[tail] * count)  10.3 us
    unnamed x15, local copies, waits for them, and re-layouts  5.3 us
    slice x1, local copies, waits for them, and re-layouts, shards(): head = patches[:reach - 1]  2.47 us
    slice x1, local copies, waits for them, and re-layouts, shards(): late = lax.ppermute(rest[reach - 1:reach], 'sec', back_by_one)  1.89 us
  transfers between devices with their start and end apart: 2, of which 1 were waited for; matrix products, arithmetic and copies ran while one was open for 3% of the time, Pallas kernels for 33%

profile of v3, /device:TPU:0, one launch (start us, length us, event | category | flops | bytes accessed | tf_op | source)
XLA Modules:
  0.0 68.3 jit_solution(16402225538802586418)
XLA Ops:
  0.6 0.0 copy-start
  0.6 2.5 %slice.83 = bf16[2,2,8,128,128]{4,3,2,1,0:T(8,128)(2,1)} slice(bf16[6,2,8,128,128]{4,3,2,1,0:T(8,128)(2,1)} %x.5), slice={[0:2], [0:2], [0:8], [0:128], [0:128]} | slice | bytes 2097152 | tf_op jit(solution)/shard_map/slice | solution.py:285
  3.1 1.3 %collective-permute-start = (bf16[2,2,8,128,128]{4,3,2,1,0:T(8,128)(2,1)}, bf16[2,2,8,128,128]{4,3,2,1,0:T(8,128)(2,1)}, u32[]{:S(2)}, u32[]{:S(2)}) collective-permute-start(bf16[2,2,8,128,128]{4,3,2,1,0:T(8,128)(2,1)} %slice.83), channel_id=1, source_target_pairs={{4,0},{8,4},{12,8},{16,12},{20,16},{24,20},{28,24},{5,1},{9,5},{13... | collective-permute-start | bytes 3145736 | tf_op jit(solution)/shard_map/ppermute | solution.py:286
  4.4 1.9 %slice.90 = bf16[1,2,8,128,128]{4,3,2,1,0:T(8,128)(2,1)} slice(bf16[6,2,8,128,128]{4,3,2,1,0:T(8,128)(2,1)} %x.5), slice={[2:3], [0:2], [0:8], [0:128], [0:128]} | slice | bytes 1048576 | tf_op jit(solution)/shard_map/slice | solution.py:288
  6.3 1.3 %collective-permute-start.1 = (bf16[1,2,8,128,128]{4,3,2,1,0:T(8,128)(2,1)}, bf16[1,2,8,128,128]{4,3,2,1,0:T(8,128)(2,1)}, u32[]{:S(2)}, u32[]{:S(2)}) collective-permute-start(bf16[1,2,8,128,128]{4,3,2,1,0:T(8,128)(2,1)} %slice.90), channel_id=1, source_target_pairs={{4,0},{8,4},{12,8},{16,12},{20,16},{24,20},{28,24},{5,1},{9,5},{13... | collective-permute-start | bytes 1572872 | tf_op jit(solution)/shard_map/ppermute | solution.py:288
  7.6 0.0 copy-done
  7.6 0.0 copy-start.1
  7.6 1.0 %copy-done.1 = bf16[784,256]{1,0:T(8,128)(2,1)S(1)} copy-done((bf16[784,256]{1,0:T(8,128)(2,1)S(1)}, bf16[784,256]{1,0:T(8,128)(2,1)}, u32[]{:S(2)}) %copy-start.1) | copy-done | bytes 401432
  8.6 0.0 copy-start.6
  8.6 0.0 copy-start.5
  8.6 19.7 %own_pairs.1 = (f32[6,3,2,8,16]{4,3,2,1,0:T(8,128)S(1)}, bf16[3,2,8,144,128]{4,3,2,1,0:T(8,128)(2,1)S(1)}) custom-call(bf16[6,2,8,128,128]{4,3,2,1,0:T(8,128)(2,1)S(1)} %copy-done, bf16[784,256]{1,0:T(8,128)(2,1)S(1)} %copy-done.1), custom_call_target="tpu_custom_call" | custom-call | flops 14495514624 | bytes 25165824 | tf_op jit(solution)/shard_map/own_pairs/pallas_call | solution.py:291
  28.3 0.0 copy-start.3
  28.3 1.2 %copy-done.3 = bf16[3,2,8,144,128]{4,3,2,1,0:T(8,128)(2,1)} copy-done((bf16[3,2,8,144,128]{4,3,2,1,0:T(8,128)(2,1)}, bf16[3,2,8,144,128]{4,3,2,1,0:T(8,128)(2,1)S(1)}, u32[]{:S(2)}) %copy-start.3) | copy-done | bytes 1769496
  29.5 0.0 copy-done.6
  29.5 0.1 convert_select_fusion
  29.6 0.1 copy.13
  29.7 0.1 reshape.44
  29.8 0.0 copy-done.5
  29.8 0.1 reshape.48
  29.9 12.8 %collective-permute-done.1.x = bf16[1,2,8,128,128]{4,3,2,1,0:T(8,128)(2,1)} collective-permute-done((bf16[1,2,8,128,128]{4,3,2,1,0:T(8,128)(2,1)}, bf16[1,2,8,128,128]{4,3,2,1,0:T(8,128)(2,1)}, u32[]{:S(2)}, u32[]{:S(2)}) %collective-permute-start.1) | collective-permute-done | bytes 524320 | tf_op jit(solution)/shard_map/ppermute | solution.py:288
  42.7 0.0 copy-start.2
  42.7 1.0 %copy-done.2 = bf16[784,256]{1,0:T(8,128)(2,1)S(1)} copy-done((bf16[784,256]{1,0:T(8,128)(2,1)S(1)}, bf16[784,256]{1,0:T(8,128)(2,1)}, u32[]{:S(2)}) %copy-start.2) | copy-done | bytes 401432
  43.7 0.0 copy-start.4
  43.7 1.5 %copy-done.4 = bf16[3,2,8,144,128]{4,3,2,1,0:T(8,128)(2,1)S(1)} copy-done((bf16[3,2,8,144,128]{4,3,2,1,0:T(8,128)(2,1)S(1)}, bf16[3,2,8,144,128]{4,3,2,1,0:T(8,128)(2,1)}, u32[]{:S(2)}) %copy-start.4) | copy-done | bytes 1769496
  45.2 2.7 %shard_map.61 = f32[1,2,8,16]{3,2,1,0:T(8,128)S(1)} custom-call(bf16[1,2,8,128,128]{4,3,2,1,0:T(8,128)(2,1)} %collective-permute-done.1.x, bf16[784,256]{1,0:T(8,128)(2,1)S(1)} %copy-done.2, bf16[3,2,8,144,128]{4,3,2,1,0:T(8,128)(2,1)S(1)} %copy-done.4), custom_call_target="tpu_custom_call" | custom-call | flops 1610612736 | bytes 4194304 | tf_op jit(solution)/shard_map/pallas_call | solution.py:337
  47.9 0.0 collective-permute-done.x
  47.9 3.5 %shard_map.60 = f32[2,2,8,16]{3,2,1,0:T(8,128)S(1)} custom-call(bf16[2,2,8,128,128]{4,3,2,1,0:T(8,128)(2,1)} %collective-permute-done.x, bf16[784,256]{1,0:T(8,128)(2,1)S(1)} %copy-done.2, bf16[3,2,8,144,128]{4,3,2,1,0:T(8,128)(2,1)S(1)} %copy-done.4, bf16[3,2,8,144,128]{4,3,2,1,0:T(8,128)(2,1)S(1)} %copy-done.4), custom_call_target="tpu_custom_call" | custom-call | flops 2415919104 | bytes 4194304 | tf_op jit(solution)/shard_map/pallas_call | solution.py:337
  51.4 4.1 %shard_map.59 = f32[3,2,8,16]{3,2,1,0:T(8,128)S(1)} custom-call(bf16[2,2,8,128,128]{4,3,2,1,0:T(8,128)(2,1)} %collective-permute-done.x, bf16[784,256]{1,0:T(8,128)(2,1)S(1)} %copy-done.2, bf16[3,2,8,144,128]{4,3,2,1,0:T(8,128)(2,1)S(1)} %copy-done.4, bf16[3,2,8,144,128]{4,3,2,1,0:T(8,128)(2,1)S(1)} %copy-done.4, bf16[3,2,8,144,128]{4,3,2,1,0:T(8,128)(2,1)S(1)} %copy-done.4), custom_call_target="tpu_custom_call" | custom-call | flops 3221225472 | bytes 4194304 | tf_op jit(solution)/shard_map/pallas_call | solution.py:337
  55.5 0.1 fusion.8
  55.7 0.1 fusion.11
  55.8 0.7 %fusion.1 = f32[2,6,3,2,8]{4,3,2,1,0:T(2,128)} fusion(f32[1,6,3,2,8]{4,3,2,1,0:T(2,128)S(1)} %bitcast.67, f32[1,6,3,2,8]{4,3,2,1,0:T(2,128)S(1)} %bitcast.69, f32[6,3]{1,0:T(8,128)S(1)} %copy.13, f32[6,3,2,8]{3,2,1,0:T(2,128)S(1)} %bitcast.65), kind=kLoop, calls=%fused_computation.2 | loop fusion | flops 2304 | bytes 5832 | tf_op jit(solution)/shard_map/mul | solution.py:357
  56.5 0.1 reshape.47
  56.6 0.1 pad_maximum_fusion
  56.6 0.1 reshape.43
  56.7 10.7 %relax.1 = f32[8,128]{1,0:T(8,128)S(1)} custom-call(f32[8,128]{1,0:T(8,128)S(1)} %pad.9.base), custom_call_target="tpu_custom_call" | custom-call | tf_op jit(solution)/shard_map/relax/pallas_call | solution.py:374
  67.5 0.1 reshape.45
  67.6 0.1 reshape.46
  67.7 0.6 copy.17
  (14 shorter events, 0.1 us)
Async XLA Ops:
  0.6 7.0 %copy-start = (bf16[6,2,8,128,128]{4,3,2,1,0:T(8,128)(2,1)S(1)}, bf16[6,2,8,128,128]{4,3,2,1,0:T(8,128)(2,1)}, u32[]{:S(2)}) copy-start(bf16[6,2,8,128,128]{4,3,2,1,0:T(8,128)(2,1)} %x.5) | copy-start | bytes 9437188
  3.1 44.8 %collective-permute-start = (bf16[2,2,8,128,128]{4,3,2,1,0:T(8,128)(2,1)}, bf16[2,2,8,128,128]{4,3,2,1,0:T(8,128)(2,1)}, u32[]{:S(2)}, u32[]{:S(2)}) collective-permute-start(bf16[2,2,8,128,128]{4,3,2,1,0:T(8,128)(2,1)} %slice.83), channel_id=1, source_target_pairs={{4,0},{8,4},{12,8},{16,12},{20,16},{24,20},{28,24},{5,1},{9,5},{13... | collective-permute-start | bytes 3145736 | tf_op jit(solution)/shard_map/ppermute | solution.py:286
  6.3 36.4 %collective-permute-start.1 = (bf16[1,2,8,128,128]{4,3,2,1,0:T(8,128)(2,1)}, bf16[1,2,8,128,128]{4,3,2,1,0:T(8,128)(2,1)}, u32[]{:S(2)}, u32[]{:S(2)}) collective-permute-start(bf16[1,2,8,128,128]{4,3,2,1,0:T(8,128)(2,1)} %slice.90), channel_id=1, source_target_pairs={{4,0},{8,4},{12,8},{16,12},{20,16},{24,20},{28,24},{5,1},{9,5},{13... | collective-permute-start | bytes 1572872 | tf_op jit(solution)/shard_map/ppermute | solution.py:288
  7.6 1.0 %copy-start.1 = (bf16[784,256]{1,0:T(8,128)(2,1)S(1)}, bf16[784,256]{1,0:T(8,128)(2,1)}, u32[]{:S(2)}) copy-start(bf16[784,256]{1,0:T(8,128)(2,1)} %constant.25.clone.tab) | copy-start | bytes 1204228
  8.6 20.9 %copy-start.6 = (s32[6,3]{0,1:T(4,128)S(1)}, s32[6,3]{0,1:T(4,128)}, u32[]{:S(2)}) copy-start(s32[6,3]{0,1:T(4,128)} %param.5) | copy-start | bytes 220
  8.6 21.2 %copy-start.5 = (f32[2,6,2,8]{3,2,1,0:T(2,128)S(1)}, f32[2,6,2,8]{3,2,1,0:T(2,128)}, u32[]{:S(2)}) copy-start(f32[2,6,2,8]{3,2,1,0:T(2,128)} %param.6) | copy-start | bytes 2308
  28.3 1.2 %copy-start.3 = (bf16[3,2,8,144,128]{4,3,2,1,0:T(8,128)(2,1)}, bf16[3,2,8,144,128]{4,3,2,1,0:T(8,128)(2,1)S(1)}, u32[]{:S(2)}) copy-start(bf16[3,2,8,144,128]{4,3,2,1,0:T(8,128)(2,1)S(1)} %get-tuple-element.6.rest_0_.rest_1_.rest_2_) | copy-start | bytes 5308420
  42.7 1.0 %copy-start.2 = (bf16[784,256]{1,0:T(8,128)(2,1)S(1)}, bf16[784,256]{1,0:T(8,128)(2,1)}, u32[]{:S(2)}) copy-start(bf16[784,256]{1,0:T(8,128)(2,1)} %constant.25.clone.tab) | copy-start | bytes 1204228
  43.7 1.5 %copy-start.4 = (bf16[3,2,8,144,128]{4,3,2,1,0:T(8,128)(2,1)S(1)}, bf16[3,2,8,144,128]{4,3,2,1,0:T(8,128)(2,1)}, u32[]{:S(2)}) copy-start(bf16[3,2,8,144,128]{4,3,2,1,0:T(8,128)(2,1)} %copy-done.3) | copy-start | bytes 5308420

commit v4 on v3

--- a/solution.py
+++ b/solution.py
@@ -116,31 +116,37 @@
     )
 
 
-def own_kernel(reach, x, tab, red, tail, spec, sums):
-    row = pl.program_id(0)
-    step = pl.program_id(1)
-    local = pl.num_programs(1)
-    cols, n = x.shape[2], x.shape[-1]
+def own_kernel(reach, x, tab, red, tail, edge, spec, sums):
+    step = pl.program_id(0)
+    local = pl.num_programs(0)
+    rows, cols, n = x.shape[1], x.shape[2], x.shape[-1]
 
     part = n // 2 + TILE
     forward, inverse = open_tables(tab, n)
 
-    def put(c, real, imag):
-        spec[step, c, :part] = real
-        spec[step, c, part:] = imag
-
-    spectra(x.at[0, 0], *forward, put)
+    for row in range(rows):
+
+        def put(c, real, imag):
+            spec[step, row, c, :part] = real
+            spec[step, row, c, part:] = imag
+
+        spectra(x.at[0, row], *forward, put)
 
     @pl.when(step >= local - reach)
     def _():
-        tail[jnp.maximum(step - (local - reach), 0), 0] = spec[step].astype(tail.dtype)
+        tail[jnp.maximum(step - (local - reach), 0)] = spec[step].astype(tail.dtype)
+
+    @pl.when(step == local - 1)
+    def _():
+        edge[0] = spec[step].astype(edge.dtype)
 
     def body(offset, carry):
-        red[step - offset, offset - 1, row] = pairs(
-            lambda c: spec[step - offset, c],
-            lambda c: spec[step, c],
-            cols, n, *inverse, sums,
-        )
+        for row in range(rows):
+            red[step - offset, offset - 1, row] = pairs(
+                lambda c: spec[step - offset, row, c],
+                lambda c: spec[step, row, c],
+                cols, n, *inverse, sums.at[row],
+            )
         return carry
 
     lax.fori_loop(1, jnp.minimum(step, reach) + 1, body, 0)
@@ -179,7 +185,9 @@
     )
 
 
-def relax_kernel(sizes, base, out, slots, field, weight, send, recv):
+def relax_kernel(
+    sizes, base, late, tab, tail, out, payload, slots, field, weight, spec, sums, send, recv
+):
     groups, tiles, local, reach, span, grid_rows, grid_cols = sizes
     half = LANES // 2
     sec = lax.axis_index("sec")
@@ -200,11 +208,36 @@
         return carry
 
     lax.fori_loop(1, count, greet, 0, unroll=unroll)
+
+    rows, cols, n = late.shape[1], late.shape[2], late.shape[-1]
+    part = n // 2 + TILE
+    forward, inverse = open_tables(tab, n)
+    for row in range(rows):
+
+        def put(c, real, imag):
+            spec[row, c, :part] = real
+            spec[row, c, part:] = imag
+
+        spectra(late.at[0, row], *forward, put)
+    payload[...] = base[...]
+    key = (local - 1) * reach + reach - 1
+    flag = base[local : local + 1, key : key + 1]
+    for row in range(rows):
+        red = pairs(
+            lambda c: tail[0, row, c].astype(jnp.float32),
+            lambda c: spec[row, c],
+            cols, n, *inverse, sums.at[row],
+        )
+        area = float(n * n)
+        scale = flag / (red[:1, cols:] / area + EPSILON)
+        at = (reach - 1) * span + row * cols
+        payload[local - 1 : local, at : at + cols] = red[:1, :cols] / area * scale
+        payload[local - 1 : local, half + at : half + at + cols] = red[1:2, cols:] / area * scale
     pl.semaphore_wait(barrier, count - 1)
 
     def copy(slot, peer):
         return pltpu.make_async_remote_copy(
-            src_ref=base,
+            src_ref=payload,
             dst_ref=slots.at[slot],
             send_sem=send.at[peer],
             recv_sem=recv.at[slot],
@@ -217,7 +250,7 @@
         return carry
 
     lax.fori_loop(1, count, start, 0, unroll=unroll)
-    slots[me] = base[...]
+    slots[me] = payload[...]
 
     def finish(d, carry):
         peer = (me + d) % count
@@ -288,33 +321,34 @@
     late = lax.ppermute(rest[reach - 1 : reach], "sec", back_by_one)
 
     patch_block = (1, 1, cols, n, n)
-    red, tail = pl.pallas_call(
+    red, tail, edge = pl.pallas_call(
         functools.partial(own_kernel, reach),
-        grid=(rows, local),
-        in_specs=[pl.BlockSpec(patch_block, lambda i, s: (s, i, 0, 0, 0))] + [fixed(tab)],
+        grid=(local,),
+        in_specs=[pl.BlockSpec((1, rows, cols, n, n), lambda s: (s, 0, 0, 0, 0))] + [fixed(tab)],
         out_specs=[
-            pl.BlockSpec((local, reach, rows, TILE, 2 * cols), lambda i, s: (0, 0, 0, 0, 0)),
-            pl.BlockSpec((reach, 1, cols, 2 * part, n), lambda i, s: (0, i, 0, 0, 0)),
+            pl.BlockSpec((local, reach, rows, TILE, 2 * cols), lambda s: (0, 0, 0, 0, 0)),
+            pl.BlockSpec((reach, rows, cols, 2 * part, n), lambda s: (0, 0, 0, 0, 0)),
+            pl.BlockSpec((1, rows, cols, 2 * part, n), lambda s: (0, 0, 0, 0, 0)),
         ],
         out_shape=[
             jax.ShapeDtypeStruct((local, reach, rows, TILE, 2 * cols), jnp.float32),
             jax.ShapeDtypeStruct((reach, rows, cols, 2 * part, n), jnp.bfloat16),
+            jax.ShapeDtypeStruct((1, rows, cols, 2 * part, n), jnp.bfloat16),
         ],
         scratch_shapes=[
-            pltpu.VMEM((local, cols, 2 * part, n), jnp.float32),
-            pltpu.VMEM((2 * cols, n), jnp.float32),
+            pltpu.VMEM((local, rows, cols, 2 * part, n), jnp.float32),
+            pltpu.VMEM((rows, 2 * cols, n), jnp.float32),
         ],
         compiler_params=pltpu.CompilerParams(
-            dimension_semantics=("arbitrary", "arbitrary"), vmem_limit_bytes=40 << 20
+            dimension_semantics=("arbitrary",), vmem_limit_bytes=40 << 20
         ),
         cost_estimate=cost(local * rows * cols, (reach * local - reach * (reach + 1) // 2) * rows * cols, n),
         name="own_pairs",
     )(patches, tab)
 
     grid = {}
-    for r in range(reach):
+    for r in range(reach - 1):
         count = reach - r
-        received, spot = (early, r) if r < reach - 1 else (late, 0)
         own_specs = [
             pl.BlockSpec((1, 1, cols, 2 * part, n), functools.partial(lambda k, i: (k, i, 0, 0, 0), k))
             for k in range(r, reach)
@@ -322,7 +356,7 @@
         far_call = pl.pallas_call(
             functools.partial(far_kernel, count),
             grid=(rows,),
-            in_specs=[pl.BlockSpec(patch_block, functools.partial(lambda k, i: (k, i, 0, 0, 0), spot))] + [fixed(tab)] + own_specs,
+            in_specs=[pl.BlockSpec(patch_block, functools.partial(lambda k, i: (k, i, 0, 0, 0), r))] + [fixed(tab)] + own_specs,
             out_specs=pl.BlockSpec((count, 1, TILE, 2 * cols), lambda i: (0, i, 0, 0)),
             out_shape=jax.ShapeDtypeStruct((count, rows, TILE, 2 * cols), jnp.float32),
             scratch_shapes=[
@@ -334,7 +368,7 @@
             ),
             cost_estimate=cost(rows * cols, count * rows * cols, n),
         )
-        far = far_call(received, tab, *([tail] * count))
+        far = far_call(early, tab, *([tail] * count))
         for item in range(count):
             section = local - reach + r + item
             grid[section, local + r - section] = far[item]
@@ -371,15 +405,17 @@
 
     sizes = (groups, tiles, local, reach, span, tiles * rows, cols)
     vmem = pl.BlockSpec(memory_space=pltpu.VMEM)
-    moved = pl.pallas_call(
+    moved, payload = pl.pallas_call(
         functools.partial(relax_kernel, sizes),
-        in_specs=[vmem],
-        out_specs=vmem,
-        out_shape=jax.ShapeDtypeStruct((TILE, LANES), jnp.float32),
+        in_specs=[vmem] * 4,
+        out_specs=[vmem, vmem],
+        out_shape=[jax.ShapeDtypeStruct((TILE, LANES), jnp.float32)] * 2,
         scratch_shapes=[
             pltpu.VMEM((groups * tiles, TILE, LANES), jnp.float32),
             pltpu.VMEM((reach + 1, groups * local, LANES), jnp.float32),
             pltpu.VMEM((reach, groups * local, LANES), jnp.float32),
+            pltpu.VMEM((rows, cols, 2 * part, n), jnp.float32),
+            pltpu.VMEM((rows, 2 * cols, n), jnp.float32),
             pltpu.SemaphoreType.DMA((groups * tiles,)),
             pltpu.SemaphoreType.DMA((groups * tiles,)),
         ],
@@ -387,7 +423,9 @@
             collective_id=0, has_side_effects=True, vmem_limit_bytes=24 << 20
         ),
         name="relax",
-    )(base)
+    )(base, late, tab, edge)
+    measured = payload[:local].reshape(local, 2, LANES // 2)[:, :, : reach * span]
+    measured = jnp.transpose(measured.reshape(local, 2, reach, rows, cols), (1, 0, 2, 3, 4))
     positions = moved[:local].reshape(local, 2, LANES // 2)[:, :, :span]
     positions = jnp.transpose(positions.reshape(local, 2, rows, cols), (1, 0, 2, 3))
     return (positions, measured)

time: 68.6 us -> 55.3 us (0.81)
  Pallas kernels: 40.7 us -> 32.1 us
  waiting for transfers between devices: 12.8 us -> 9.06 us
  other arithmetic: 1.17 us -> 0.47 us
    ppermute x1, waiting for transfers between devices: 12.8 us -> 2.65 us  [shards(): late = lax.ppermute(rest[reach - 1:reach], 'sec', back_by_one)]
    pallas_call x5 -> x4, Pallas kernels: 40.7 us -> 32.1 us  [the longest x1 15.5 us: shards(): pl.pallas_call(functools.partial(own_kernel, reach), grid=(local,), in_sp...]
    ppermute x1, waiting for transfers between devices: 0.01 us -> 6.4 us  [shards(): early = lax.ppermute(head, 'sec', back_by_one)]
    slice x1, local copies, waits for them, and re-layouts: 1.89 us -> 1.08 us  [shards(): late = lax.ppermute(rest[reach - 1:reach], 'sec', back_by_one)]
    mul x1 -> x0, other arithmetic: 0.71 us -> none  [shards(): measured = ratio * weights[None, :, :, None, None]]
    unnamed x15 -> x14, local copies, waits for them, and re-layouts: 5.3 us -> 5.84 us
  transfers between devices with their start and end apart: 2 -> 2, of which waited for: 1 -> 2; matrix products, arithmetic and copies ran while one was open for 3% -> 4% of each run, Pallas kernels for 33% -> 38%
where the time goes in v4:
time: 55.3 us; the launch traced here: 55 us
  Pallas kernels  32.1 us (58%)
  local copies, waits for them, and re-layouts  10.1 us (18%)
  waiting for transfers between devices  9.06 us (16%)
  starting transfers between devices  2.57 us (5%)
  between operations  0.77 us (1%)
    pallas_call x1, Pallas kernels, shards(): pl.pallas_call(functools.partial(own_kernel, reach), grid=(local,), in_sp...  15.5 us
    pallas_call x1, Pallas kernels, shards(): pl.pallas_call(functools.partial(relax_kernel, sizes), in_specs=[vmem] *...  11 us
    ppermute x1, waiting for transfers between devices, shards(): early = lax.ppermute(head, 'sec', back_by_one)  6.4 us
    unnamed x14, local copies, waits for them, and re-layouts  5.84 us
    pallas_call x2, Pallas kernels, shards(): far = far_call(early, tab, *[tail] * count)  5.65 us
    ppermute x1, waiting for transfers between devices, shards(): late = lax.ppermute(rest[reach - 1:reach], 'sec', back_by_one)  2.65 us
    slice x1, local copies, waits for them, and re-layouts, shards(): head = patches[:reach - 1]  2.37 us
    ppermute x1, starting transfers between devices, shards(): late = lax.ppermute(rest[reach - 1:reach], 'sec', back_by_one)  1.29 us
  transfers between devices with their start and end apart: 2, of which 2 were waited for; matrix products, arithmetic and copies ran while one was open for 4% of the time, Pallas kernels for 38%

profile of v4, /device:TPU:0, one launch (start us, length us, event | category | flops | bytes accessed | tf_op | source)
XLA Modules:
  0.0 55.0 jit_solution(13626721035132036533)
XLA Ops:
  0.6 0.0 copy-start.1
  0.6 2.4 %slice.92 = bf16[2,2,8,128,128]{4,3,2,1,0:T(8,128)(2,1)} slice(bf16[6,2,8,128,128]{4,3,2,1,0:T(8,128)(2,1)} %x.5), slice={[0:2], [0:2], [0:8], [0:128], [0:128]} | slice | bytes 2097152 | tf_op jit(solution)/shard_map/slice | solution.py:318
  3.0 1.3 %collective-permute-start = (bf16[2,2,8,128,128]{4,3,2,1,0:T(8,128)(2,1)}, bf16[2,2,8,128,128]{4,3,2,1,0:T(8,128)(2,1)S(1)}, u32[]{:S(2)}, u32[]{:S(2)}) collective-permute-start(bf16[2,2,8,128,128]{4,3,2,1,0:T(8,128)(2,1)} %slice.92), channel_id=1, source_target_pairs={{4,0},{8,4},{12,8},{16,12},{20,16},{24,20},{28,24},{5,1},{9,5},{13... | collective-permute-start | bytes 3145736 | tf_op jit(solution)/shard_map/ppermute | solution.py:319
  4.3 1.1 %slice.103 = bf16[1,2,8,128,128]{4,3,2,1,0:T(8,128)(2,1)S(1)} slice(bf16[6,2,8,128,128]{4,3,2,1,0:T(8,128)(2,1)} %x.5), slice={[2:3], [0:2], [0:8], [0:128], [0:128]} | slice | bytes 1048576 | tf_op jit(solution)/shard_map/slice | solution.py:321
  5.4 1.3 %collective-permute-start.1 = (bf16[1,2,8,128,128]{4,3,2,1,0:T(8,128)(2,1)S(1)}, bf16[1,2,8,128,128]{4,3,2,1,0:T(8,128)(2,1)S(1)}, u32[]{:S(2)}, u32[]{:S(2)}) collective-permute-start(bf16[1,2,8,128,128]{4,3,2,1,0:T(8,128)(2,1)S(1)} %slice.103), channel_id=1, source_target_pairs={{4,0},{8,4},{12,8},{16,12},{20,16},{24,20},{28,24},{5,1},{9,5},{13... | collective-permute-start | bytes 1572872 | tf_op jit(solution)/shard_map/ppermute | solution.py:321
  6.7 0.0 copy-done.1
  6.7 0.0 copy-start
  6.7 1.9 %copy-done = bf16[6,2,8,128,128]{4,3,2,1,0:T(8,128)(2,1)S(1)} copy-done((bf16[6,2,8,128,128]{4,3,2,1,0:T(8,128)(2,1)S(1)}, bf16[6,2,8,128,128]{4,3,2,1,0:T(8,128)(2,1)}, u32[]{:S(2)}) %copy-start) | copy-done | bytes 3145752
  8.6 0.0 copy-start.5
  8.6 0.0 copy-start.4
  8.6 15.5 %own_pairs.1 = (f32[6,3,2,8,16]{4,3,2,1,0:T(8,128)S(1)}, bf16[3,2,8,144,128]{4,3,2,1,0:T(8,128)(2,1)S(1)}, bf16[1,2,8,144,128]{4,3,2,1,0:T(8,128)(2,1)S(1)}) custom-call(bf16[6,2,8,128,128]{4,3,2,1,0:T(8,128)(2,1)S(1)} %copy-done, bf16[784,256]{1,0:T(8,128)(2,1)S(1)} %copy-done.1), custom_call_target="tpu_custom_call" | custom-call | flops 14495514624 | bytes 25165824 | tf_op jit(solution)/shard_map/own_pairs/pallas_call | solution.py:324
  24.1 0.0 copy-start.2
  24.1 1.2 %copy-done.2 = bf16[3,2,8,144,128]{4,3,2,1,0:T(8,128)(2,1)} copy-done((bf16[3,2,8,144,128]{4,3,2,1,0:T(8,128)(2,1)}, bf16[3,2,8,144,128]{4,3,2,1,0:T(8,128)(2,1)S(1)}, u32[]{:S(2)}) %copy-start.2) | copy-done | bytes 1769496
  25.3 0.0 copy-done.5
  25.3 0.1 convert_select_fusion
  25.4 0.1 copy.14
  25.5 0.1 reshape.50
  25.6 0.0 copy-done.4
  25.6 0.1 reshape.56
  25.7 6.4 %collective-permute-done.x = bf16[2,2,8,128,128]{4,3,2,1,0:T(8,128)(2,1)S(1)} collective-permute-done((bf16[2,2,8,128,128]{4,3,2,1,0:T(8,128)(2,1)}, bf16[2,2,8,128,128]{4,3,2,1,0:T(8,128)(2,1)S(1)}, u32[]{:S(2)}, u32[]{:S(2)}) %collective-permute-start) | collective-permute-done | bytes 1048608 | tf_op jit(solution)/shard_map/ppermute | solution.py:319
  32.1 0.0 copy-start.3
  32.1 1.5 %copy-done.3 = bf16[3,2,8,144,128]{4,3,2,1,0:T(8,128)(2,1)S(1)} copy-done((bf16[3,2,8,144,128]{4,3,2,1,0:T(8,128)(2,1)S(1)}, bf16[3,2,8,144,128]{4,3,2,1,0:T(8,128)(2,1)}, u32[]{:S(2)}) %copy-start.3) | copy-done | bytes 1769496
  33.6 2.5 %shard_map.60 = f32[2,2,8,16]{3,2,1,0:T(8,128)S(1)} custom-call(bf16[2,2,8,128,128]{4,3,2,1,0:T(8,128)(2,1)S(1)} %collective-permute-done.x, bf16[784,256]{1,0:T(8,128)(2,1)S(1)} %copy-done.1, bf16[3,2,8,144,128]{4,3,2,1,0:T(8,128)(2,1)S(1)} %copy-done.3, bf16[3,2,8,144,128]{4,3,2,1,0:T(8,128)(2,1)S(1)} %copy-done.3), custom_call_target="tpu_custom_call" | custom-call | flops 2415919104 | bytes 4194304 | tf_op jit(solution)/shard_map/pallas_call | solution.py:371
  36.1 3.1 %shard_map.59 = f32[3,2,8,16]{3,2,1,0:T(8,128)S(1)} custom-call(bf16[2,2,8,128,128]{4,3,2,1,0:T(8,128)(2,1)S(1)} %collective-permute-done.x, bf16[784,256]{1,0:T(8,128)(2,1)S(1)} %copy-done.1, bf16[3,2,8,144,128]{4,3,2,1,0:T(8,128)(2,1)S(1)} %copy-done.3, bf16[3,2,8,144,128]{4,3,2,1,0:T(8,128)(2,1)S(1)} %copy-done.3, bf16[3,2,8,144,128]{4,3,2,1,0:T(8,128)(2,1)S(1)} %copy-done.3), custom_call_target="tpu_custom_call" | custom-call | flops 3221225472 | bytes 4194304 | tf_op jit(solution)/shard_map/pallas_call | solution.py:371
  39.3 0.1 fusion.9
  39.5 0.1 fusion.2
  39.6 0.1 reshape.55
  39.7 0.1 pad_maximum_fusion
  39.7 0.1 reshape.49
  39.8 2.7 %collective-permute-done.1.late = bf16[1,2,8,128,128]{4,3,2,1,0:T(8,128)(2,1)S(1)} collective-permute-done((bf16[1,2,8,128,128]{4,3,2,1,0:T(8,128)(2,1)S(1)}, bf16[1,2,8,128,128]{4,3,2,1,0:T(8,128)(2,1)S(1)}, u32[]{:S(2)}, u32[]{:S(2)}) %collective-permute-start.1) | collective-permute-done | bytes 524320 | tf_op jit(solution)/shard_map/ppermute | solution.py:321
  42.5 11.0 %relax.1 = (f32[8,128]{1,0:T(8,128)S(1)}, f32[8,128]{1,0:T(8,128)S(1)}) custom-call(f32[8,128]{1,0:T(8,128)S(1)} %pad.9.base, bf16[1,2,8,128,128]{4,3,2,1,0:T(8,128)(2,1)S(1)} %collective-permute-done.1.late, bf16[784,256]{1,0:T(8,128)(2,1)S(1)} %copy-done.1, bf16[1,2,8,144,128]{4,3,2,1,0:T(8,128)(2,1)S(1)} %get-tuple-element.11.tail), custom_call_target="tpu_custom_call" | custom-call | tf_op jit(solution)/shard_map/relax/pallas_call | solution.py:408
  53.5 0.1 reshape.53
  53.5 0.1 reshape.51
  53.6 0.1 reshape.52
  53.7 0.6 %copy.18 = f32[2,6,2,8]{3,2,1,0:T(2,128)} copy(f32[2,6,2,8]{3,2,0,1:T(2,128)S(1)} %bitcast.74) | data formatting | bytes 1536
  54.3 0.1 reshape.54
  54.4 0.6 %copy.19 = f32[2,6,3,2,8]{4,3,2,1,0:T(2,128)} copy(f32[2,6,3,2,8]{4,3,2,0,1:T(2,128)S(1)} %bitcast.70) | data formatting | bytes 4608
  (14 shorter events, 0.1 us)
Async XLA Ops:
  0.6 6.1 %copy-start.1 = (bf16[784,256]{1,0:T(8,128)(2,1)S(1)}, bf16[784,256]{1,0:T(8,128)(2,1)}, u32[]{:S(2)}) copy-start(bf16[784,256]{1,0:T(8,128)(2,1)} %constant.25.clone.tab) | copy-start | bytes 1204228
  3.0 29.1 %collective-permute-start = (bf16[2,2,8,128,128]{4,3,2,1,0:T(8,128)(2,1)}, bf16[2,2,8,128,128]{4,3,2,1,0:T(8,128)(2,1)S(1)}, u32[]{:S(2)}, u32[]{:S(2)}) collective-permute-start(bf16[2,2,8,128,128]{4,3,2,1,0:T(8,128)(2,1)} %slice.92), channel_id=1, source_target_pairs={{4,0},{8,4},{12,8},{16,12},{20,16},{24,20},{28,24},{5,1},{9,5},{13... | collective-permute-start | bytes 3145736 | tf_op jit(solution)/shard_map/ppermute | solution.py:319
  5.4 37.1 %collective-permute-start.1 = (bf16[1,2,8,128,128]{4,3,2,1,0:T(8,128)(2,1)S(1)}, bf16[1,2,8,128,128]{4,3,2,1,0:T(8,128)(2,1)S(1)}, u32[]{:S(2)}, u32[]{:S(2)}) collective-permute-start(bf16[1,2,8,128,128]{4,3,2,1,0:T(8,128)(2,1)S(1)} %slice.103), channel_id=1, source_target_pairs={{4,0},{8,4},{12,8},{16,12},{20,16},{24,20},{28,24},{5,1},{9,5},{13... | collective-permute-start | bytes 1572872 | tf_op jit(solution)/shard_map/ppermute | solution.py:321
  6.7 1.9 %copy-start = (bf16[6,2,8,128,128]{4,3,2,1,0:T(8,128)(2,1)S(1)}, bf16[6,2,8,128,128]{4,3,2,1,0:T(8,128)(2,1)}, u32[]{:S(2)}) copy-start(bf16[6,2,8,128,128]{4,3,2,1,0:T(8,128)(2,1)} %x.5) | copy-start | bytes 9437188
  8.6 16.7 %copy-start.5 = (s32[6,3]{0,1:T(4,128)S(1)}, s32[6,3]{0,1:T(4,128)}, u32[]{:S(2)}) copy-start(s32[6,3]{0,1:T(4,128)} %param.5) | copy-start | bytes 220
  8.6 17.0 %copy-start.4 = (f32[2,6,2,8]{3,2,1,0:T(2,128)S(1)}, f32[2,6,2,8]{3,2,1,0:T(2,128)}, u32[]{:S(2)}) copy-start(f32[2,6,2,8]{3,2,1,0:T(2,128)} %param.6) | copy-start | bytes 2308
  24.1 1.2 %copy-start.2 = (bf16[3,2,8,144,128]{4,3,2,1,0:T(8,128)(2,1)}, bf16[3,2,8,144,128]{4,3,2,1,0:T(8,128)(2,1)S(1)}, u32[]{:S(2)}) copy-start(bf16[3,2,8,144,128]{4,3,2,1,0:T(8,128)(2,1)S(1)} %get-tuple-element.9.rest_0_.rest_1_.rest_2_) | copy-start | bytes 5308420
  32.1 1.5 %copy-start.3 = (bf16[3,2,8,144,128]{4,3,2,1,0:T(8,128)(2,1)S(1)}, bf16[3,2,8,144,128]{4,3,2,1,0:T(8,128)(2,1)}, u32[]{:S(2)}) copy-start(bf16[3,2,8,144,128]{4,3,2,1,0:T(8,128)(2,1)} %copy-done.2) | copy-start | bytes 5308420

commit v5 on v4

--- a/solution.py
+++ b/solution.py
@@ -186,7 +186,7 @@
 
 
 def relax_kernel(
-    sizes, base, late, tab, tail, out, payload, slots, field, weight, spec, sums, send, recv
+    sizes, base, late, tab, edge, out, payload, slots, field, weight, spec, tail, sums, local_sem, send, recv
 ):
     groups, tiles, local, reach, span, grid_rows, grid_cols = sizes
     half = LANES // 2
@@ -199,6 +199,8 @@
     def place(index):
         return (index // tiles, index % tiles)
 
+    fetch = pltpu.make_async_copy(edge, tail, local_sem)
+    fetch.start()
     barrier = pltpu.get_barrier_semaphore()
 
     def greet(d, carry):
@@ -219,6 +221,7 @@
             spec[row, c, part:] = imag
 
         spectra(late.at[0, row], *forward, put)
+    fetch.wait()
     payload[...] = base[...]
     key = (local - 1) * reach + reach - 1
     flag = base[local : local + 1, key : key + 1]
@@ -315,13 +318,15 @@
     part = n // 2 + TILE
     tab = jnp.asarray(tables(n))
     back_by_one = [(i, i - 1) for i in range(1, groups)]
-    head = patches[: reach - 1]
-    early = lax.ppermute(head, "sec", back_by_one)
-    _, rest = lax.optimization_barrier((head, patches))
-    late = lax.ppermute(rest[reach - 1 : reach], "sec", back_by_one)
+    ahead = []
+    source = patches
+    for r in range(reach):
+        piece = source[r : r + 1]
+        ahead.append(lax.ppermute(piece, "sec", back_by_one))
+        _, source = lax.optimization_barrier((piece, source))
 
     patch_block = (1, 1, cols, n, n)
-    red, tail, edge = pl.pallas_call(
+    own_call = pl.pallas_call(
         functools.partial(own_kernel, reach),
         grid=(local,),
         in_specs=[pl.BlockSpec((1, rows, cols, n, n), lambda s: (s, 0, 0, 0, 0))] + [fixed(tab)],
@@ -344,7 +349,8 @@
         ),
         cost_estimate=cost(local * rows * cols, (reach * local - reach * (reach + 1) // 2) * rows * cols, n),
         name="own_pairs",
-    )(patches, tab)
+    )
+    red, tail, edge = own_call(patches, tab)
 
     grid = {}
     for r in range(reach - 1):
@@ -356,7 +362,7 @@
         far_call = pl.pallas_call(
             functools.partial(far_kernel, count),
             grid=(rows,),
-            in_specs=[pl.BlockSpec(patch_block, functools.partial(lambda k, i: (k, i, 0, 0, 0), r))] + [fixed(tab)] + own_specs,
+            in_specs=[pl.BlockSpec(patch_block, lambda i: (0, i, 0, 0, 0))] + [fixed(tab)] + own_specs,
             out_specs=pl.BlockSpec((count, 1, TILE, 2 * cols), lambda i: (0, i, 0, 0)),
             out_shape=jax.ShapeDtypeStruct((count, rows, TILE, 2 * cols), jnp.float32),
             scratch_shapes=[
@@ -368,7 +374,7 @@
             ),
             cost_estimate=cost(rows * cols, count * rows * cols, n),
         )
-        far = far_call(early, tab, *([tail] * count))
+        far = far_call(ahead[r], tab, *([tail] * count))
         for item in range(count):
             section = local - reach + r + item
             grid[section, local + r - section] = far[item]
@@ -407,7 +413,7 @@
     vmem = pl.BlockSpec(memory_space=pltpu.VMEM)
     moved, payload = pl.pallas_call(
         functools.partial(relax_kernel, sizes),
-        in_specs=[vmem] * 4,
+        in_specs=[vmem] * 3 + [pl.BlockSpec(memory_space=pltpu.HBM)],
         out_specs=[vmem, vmem],
         out_shape=[jax.ShapeDtypeStruct((TILE, LANES), jnp.float32)] * 2,
         scratch_shapes=[
@@ -415,7 +421,9 @@
             pltpu.VMEM((reach + 1, groups * local, LANES), jnp.float32),
             pltpu.VMEM((reach, groups * local, LANES), jnp.float32),
             pltpu.VMEM((rows, cols, 2 * part, n), jnp.float32),
+            pltpu.VMEM((1, rows, cols, 2 * part, n), jnp.bfloat16),
             pltpu.VMEM((rows, 2 * cols, n), jnp.float32),
+            pltpu.SemaphoreType.DMA,
             pltpu.SemaphoreType.DMA((groups * tiles,)),
             pltpu.SemaphoreType.DMA((groups * tiles,)),
         ],
@@ -423,7 +431,7 @@
             collective_id=0, has_side_effects=True, vmem_limit_bytes=24 << 20
         ),
         name="relax",
-    )(base, late, tab, edge)
+    )(base, ahead[-1], tab, edge)
     measured = payload[:local].reshape(local, 2, LANES // 2)[:, :, : reach * span]
     measured = jnp.transpose(measured.reshape(local, 2, reach, rows, cols), (1, 0, 2, 3, 4))
     positions = moved[:local].reshape(local, 2, LANES // 2)[:, :, :span]

time: 55.3 us -> 55.5 us (level)
  waiting for transfers between devices: 9.06 us -> 6.73 us
  starting transfers between devices: 2.57 us -> 3.85 us
  local copies, waits for them, and re-layouts: 10.1 us -> 10.8 us
    ppermute x2 -> x3, waiting for transfers between devices: 9.06 us -> 6.73 us  [shards(): ahead.append(lax.ppermute(piece, 'sec', back_by_one))]
    slice x2 -> x3, local copies, waits for them, and re-layouts: 3.45 us -> 5.01 us  [shards(): piece = source[r:r + 1]]
    ppermute x2 -> x3, starting transfers between devices: 2.57 us -> 3.85 us  [shards(): ahead.append(lax.ppermute(piece, 'sec', back_by_one))]
    unnamed x14 -> x16, local copies, waits for them, and re-layouts: 5.84 us -> 4.97 us
  transfers between devices with their start and end apart: 2 -> 3, of which waited for: 2 -> 1; matrix products, arithmetic and copies ran while one was open for 4% -> 7% of each run, Pallas kernels for 38% -> 38%
where the time goes in v5:
time: 55.5 us; the launch traced here: 55.1 us
  Pallas kernels  32.5 us (59%)
  local copies, waits for them, and re-layouts  10.8 us (19%)
  waiting for transfers between devices  6.73 us (12%)
  starting transfers between devices  3.85 us (7%)
  between operations  0.81 us (1%)
    pallas_call x1, Pallas kernels, shards(): red, tail, edge = own_call(patches, tab)  15.5 us
    pallas_call x1, Pallas kernels, shards(): pl.pallas_call(functools.partial(relax_kernel, sizes), in_specs=[vmem] *...  11.4 us
    ppermute x3, waiting for transfers between devices, shards(): ahead.append(lax.ppermute(piece, 'sec', back_by_one))  6.73 us
    pallas_call x2, Pallas kernels, shards(): far = far_call(ahead[r], tab, *[tail] * count)  5.66 us
    slice x3, local copies, waits for them, and re-layouts, shards(): piece = source[r:r + 1]  5.01 us
    unnamed x16, local copies, waits for them, and re-layouts  4.97 us
    ppermute x3, starting transfers between devices, shards(): ahead.append(lax.ppermute(piece, 'sec', back_by_one))  3.85 us
  transfers between devices with their start and end apart: 3, of which 1 were waited for; matrix products, arithmetic and copies ran while one was open for 7% of the time, Pallas kernels for 38%

profile of v5, /device:TPU:0, one launch (start us, length us, event | category | flops | bytes accessed | tf_op | source)
XLA Modules:
  0.0 55.1 jit_solution(5865911810242996268)
XLA Ops:
  0.6 0.0 copy-start
  0.6 2.0 %slice.95 = bf16[1,2,8,128,128]{4,3,2,1,0:T(8,128)(2,1)} slice(bf16[6,2,8,128,128]{4,3,2,1,0:T(8,128)(2,1)} %x.5), slice={[0:1], [0:2], [0:8], [0:128], [0:128]} | slice | bytes 1048576 | tf_op jit(solution)/shard_map/slice | solution.py:324
  2.7 1.3 %collective-permute-start = (bf16[1,2,8,128,128]{4,3,2,1,0:T(8,128)(2,1)}, bf16[1,2,8,128,128]{4,3,2,1,0:T(8,128)(2,1)S(1)}, u32[]{:S(2)}, u32[]{:S(2)}) collective-permute-start(bf16[1,2,8,128,128]{4,3,2,1,0:T(8,128)(2,1)} %slice.95), channel_id=1, source_target_pairs={{4,0},{8,4},{12,8},{16,12},{20,16},{24,20},{28,24},{5,1},{9,5},{13... | collective-permute-start | bytes 1572872 | tf_op jit(solution)/shard_map/ppermute | solution.py:325
  4.0 1.9 %slice.99 = bf16[1,2,8,128,128]{4,3,2,1,0:T(8,128)(2,1)} slice(bf16[6,2,8,128,128]{4,3,2,1,0:T(8,128)(2,1)} %x.5), slice={[1:2], [0:2], [0:8], [0:128], [0:128]} | slice | bytes 1048576 | tf_op jit(solution)/shard_map/slice | solution.py:324
  5.9 1.3 %collective-permute-start.1 = (bf16[1,2,8,128,128]{4,3,2,1,0:T(8,128)(2,1)}, bf16[1,2,8,128,128]{4,3,2,1,0:T(8,128)(2,1)S(1)}, u32[]{:S(2)}, u32[]{:S(2)}) collective-permute-start(bf16[1,2,8,128,128]{4,3,2,1,0:T(8,128)(2,1)} %slice.99), channel_id=1, source_target_pairs={{4,0},{8,4},{12,8},{16,12},{20,16},{24,20},{28,24},{5,1},{9,5},{13... | collective-permute-start | bytes 1572872 | tf_op jit(solution)/shard_map/ppermute | solution.py:325
  7.1 1.1 %slice.107 = bf16[1,2,8,128,128]{4,3,2,1,0:T(8,128)(2,1)S(1)} slice(bf16[6,2,8,128,128]{4,3,2,1,0:T(8,128)(2,1)} %x.5), slice={[2:3], [0:2], [0:8], [0:128], [0:128]} | slice | bytes 1048576 | tf_op jit(solution)/shard_map/slice | solution.py:324
  8.2 1.3 %collective-permute-start.2 = (bf16[1,2,8,128,128]{4,3,2,1,0:T(8,128)(2,1)S(1)}, bf16[1,2,8,128,128]{4,3,2,1,0:T(8,128)(2,1)S(1)}, u32[]{:S(2)}, u32[]{:S(2)}) collective-permute-start(bf16[1,2,8,128,128]{4,3,2,1,0:T(8,128)(2,1)S(1)} %slice.107), channel_id=1, source_target_pairs={{4,0},{8,4},{12,8},{16,12},{20,16},{24,20},{28,24},{5,1},{9,5},{13... | collective-permute-start | bytes 1572872 | tf_op jit(solution)/shard_map/ppermute | solution.py:325
  9.5 0.0 copy-done
  9.6 0.0 copy-start.1
  9.6 1.0 %copy-done.1 = bf16[784,256]{1,0:T(8,128)(2,1)S(1)} copy-done((bf16[784,256]{1,0:T(8,128)(2,1)S(1)}, bf16[784,256]{1,0:T(8,128)(2,1)}, u32[]{:S(2)}) %copy-start.1) | copy-done | bytes 401432
  10.6 0.0 copy-start.6
  10.6 0.0 copy-start.5
  10.6 0.0 copy-start.2
  10.6 15.5 %own_pairs.1 = (f32[6,3,2,8,16]{4,3,2,1,0:T(8,128)S(1)}, bf16[3,2,8,144,128]{4,3,2,1,0:T(8,128)(2,1)S(1)}, bf16[1,2,8,144,128]{4,3,2,1,0:T(8,128)(2,1)S(1)}) custom-call(bf16[6,2,8,128,128]{4,3,2,1,0:T(8,128)(2,1)S(1)} %copy-done, bf16[784,256]{1,0:T(8,128)(2,1)S(1)} %copy-done.1), custom_call_target="tpu_custom_call" | custom-call | flops 14495514624 | bytes 25165824 | tf_op jit(solution)/shard_map/own_pairs/pallas_call | solution.py:353
  26.0 0.0 copy-start.3
  26.0 1.3 %copy-done.3 = bf16[3,2,8,144,128]{4,3,2,1,0:T(8,128)(2,1)} copy-done((bf16[3,2,8,144,128]{4,3,2,1,0:T(8,128)(2,1)}, bf16[3,2,8,144,128]{4,3,2,1,0:T(8,128)(2,1)S(1)}, u32[]{:S(2)}) %copy-start.3) | copy-done | bytes 1769496
  27.3 0.0 copy-done.6
  27.3 0.1 convert_select_fusion
  27.4 0.1 copy.14
  27.5 0.0 copy-done.5
  27.5 0.1 reshape.56
  27.6 0.1 reshape.50
  27.7 0.0 collective-permute-done.x
  27.7 0.0 copy-done.2
  27.7 0.0 copy-start.4
  27.7 1.5 %copy-done.4 = bf16[3,2,8,144,128]{4,3,2,1,0:T(8,128)(2,1)S(1)} copy-done((bf16[3,2,8,144,128]{4,3,2,1,0:T(8,128)(2,1)S(1)}, bf16[3,2,8,144,128]{4,3,2,1,0:T(8,128)(2,1)}, u32[]{:S(2)}) %copy-start.4) | copy-done | bytes 1769496
  29.2 3.1 %shard_map.59 = f32[3,2,8,16]{3,2,1,0:T(8,128)S(1)} custom-call(bf16[1,2,8,128,128]{4,3,2,1,0:T(8,128)(2,1)S(1)} %collective-permute-done.x, bf16[784,256]{1,0:T(8,128)(2,1)S(1)} %copy-done.2, bf16[3,2,8,144,128]{4,3,2,1,0:T(8,128)(2,1)S(1)} %copy-done.4, bf16[3,2,8,144,128]{4,3,2,1,0:T(8,128)(2,1)S(1)} %copy-done.4, bf16[3,2,8,144,128]{4,3,2,1,0:T(8,128)(2,1)S(1)} %copy-done.4), custom_call_target="tpu_custom_call" | custom-call | flops 3221225472 | bytes 4194304 | tf_op jit(solution)/shard_map/pallas_call | solution.py:377
  32.3 0.0 collective-permute-done.1.x
  32.3 2.6 %shard_map.60 = f32[2,2,8,16]{3,2,1,0:T(8,128)S(1)} custom-call(bf16[1,2,8,128,128]{4,3,2,1,0:T(8,128)(2,1)S(1)} %collective-permute-done.1.x, bf16[784,256]{1,0:T(8,128)(2,1)S(1)} %copy-done.2, bf16[3,2,8,144,128]{4,3,2,1,0:T(8,128)(2,1)S(1)} %copy-done.4, bf16[3,2,8,144,128]{4,3,2,1,0:T(8,128)(2,1)S(1)} %copy-done.4), custom_call_target="tpu_custom_call" | custom-call | flops 2415919104 | bytes 4194304 | tf_op jit(solution)/shard_map/pallas_call | solution.py:377
  34.9 0.1 fusion.9
  35.1 0.1 fusion.2
  35.2 0.1 reshape.55
  35.3 0.1 pad_maximum_fusion
  35.3 0.1 reshape.49
  35.4 6.7 %collective-permute-done.2.late = bf16[1,2,8,128,128]{4,3,2,1,0:T(8,128)(2,1)S(1)} collective-permute-done((bf16[1,2,8,128,128]{4,3,2,1,0:T(8,128)(2,1)S(1)}, bf16[1,2,8,128,128]{4,3,2,1,0:T(8,128)(2,1)S(1)}, u32[]{:S(2)}, u32[]{:S(2)}) %collective-permute-start.2) | collective-permute-done | bytes 524320 | tf_op jit(solution)/shard_map/ppermute | solution.py:325
  42.2 11.4 %relax.1 = (f32[8,128]{1,0:T(8,128)S(1)}, f32[8,128]{1,0:T(8,128)S(1)}) custom-call(f32[8,128]{1,0:T(8,128)S(1)} %pad.9.base, bf16[1,2,8,128,128]{4,3,2,1,0:T(8,128)(2,1)S(1)} %collective-permute-done.2.late, bf16[784,256]{1,0:T(8,128)(2,1)S(1)} %copy-done.2, bf16[1,2,8,144,128]{4,3,2,1,0:T(8,128)(2,1)S(1)} %get-tuple-element.13.edge), custom_call_target="tpu_custom_call" | custom-call | tf_op jit(solution)/shard_map/relax/pallas_call | solution.py:414
  53.5 0.1 reshape.53
  53.6 0.1 reshape.54
  53.7 0.6 %copy.19 = f32[2,6,3,2,8]{4,3,2,1,0:T(2,128)} copy(f32[2,6,3,2,8]{4,3,2,0,1:T(2,128)S(1)} %bitcast.70) | data formatting | bytes 4608
  54.4 0.1 reshape.51
  54.4 0.1 reshape.52
  54.5 0.6 %copy.18 = f32[2,6,2,8]{3,2,1,0:T(2,128)} copy(f32[2,6,2,8]{3,2,0,1:T(2,128)S(1)} %bitcast.74) | data formatting | bytes 1536
  (15 shorter events, 0.1 us)
Async XLA Ops:
  0.6 8.9 %copy-start = (bf16[6,2,8,128,128]{4,3,2,1,0:T(8,128)(2,1)S(1)}, bf16[6,2,8,128,128]{4,3,2,1,0:T(8,128)(2,1)}, u32[]{:S(2)}) copy-start(bf16[6,2,8,128,128]{4,3,2,1,0:T(8,128)(2,1)} %x.5) | copy-start | bytes 9437188
  2.7 25.0 %collective-permute-start = (bf16[1,2,8,128,128]{4,3,2,1,0:T(8,128)(2,1)}, bf16[1,2,8,128,128]{4,3,2,1,0:T(8,128)(2,1)S(1)}, u32[]{:S(2)}, u32[]{:S(2)}) collective-permute-start(bf16[1,2,8,128,128]{4,3,2,1,0:T(8,128)(2,1)} %slice.95), channel_id=1, source_target_pairs={{4,0},{8,4},{12,8},{16,12},{20,16},{24,20},{28,24},{5,1},{9,5},{13... | collective-permute-start | bytes 1572872 | tf_op jit(solution)/shard_map/ppermute | solution.py:325
  5.9 26.5 %collective-permute-start.1 = (bf16[1,2,8,128,128]{4,3,2,1,0:T(8,128)(2,1)}, bf16[1,2,8,128,128]{4,3,2,1,0:T(8,128)(2,1)S(1)}, u32[]{:S(2)}, u32[]{:S(2)}) collective-permute-start(bf16[1,2,8,128,128]{4,3,2,1,0:T(8,128)(2,1)} %slice.99), channel_id=1, source_target_pairs={{4,0},{8,4},{12,8},{16,12},{20,16},{24,20},{28,24},{5,1},{9,5},{13... | collective-permute-start | bytes 1572872 | tf_op jit(solution)/shard_map/ppermute | solution.py:325
  8.2 33.9 %collective-permute-start.2 = (bf16[1,2,8,128,128]{4,3,2,1,0:T(8,128)(2,1)S(1)}, bf16[1,2,8,128,128]{4,3,2,1,0:T(8,128)(2,1)S(1)}, u32[]{:S(2)}, u32[]{:S(2)}) collective-permute-start(bf16[1,2,8,128,128]{4,3,2,1,0:T(8,128)(2,1)S(1)} %slice.107), channel_id=1, source_target_pairs={{4,0},{8,4},{12,8},{16,12},{20,16},{24,20},{28,24},{5,1},{9,5},{13... | collective-permute-start | bytes 1572872 | tf_op jit(solution)/shard_map/ppermute | solution.py:325
  9.6 1.0 %copy-start.1 = (bf16[784,256]{1,0:T(8,128)(2,1)S(1)}, bf16[784,256]{1,0:T(8,128)(2,1)}, u32[]{:S(2)}) copy-start(bf16[784,256]{1,0:T(8,128)(2,1)} %constant.25.clone.tab) | copy-start | bytes 1204228
  10.6 16.7 %copy-start.6 = (s32[6,3]{0,1:T(4,128)S(1)}, s32[6,3]{0,1:T(4,128)}, u32[]{:S(2)}) copy-start(s32[6,3]{0,1:T(4,128)} %param.5) | copy-start | bytes 220
  10.6 16.9 %copy-start.5 = (f32[2,6,2,8]{3,2,1,0:T(2,128)S(1)}, f32[2,6,2,8]{3,2,1,0:T(2,128)}, u32[]{:S(2)}) copy-start(f32[2,6,2,8]{3,2,1,0:T(2,128)} %param.6) | copy-start | bytes 2308
  10.6 17.1 %copy-start.2 = (bf16[784,256]{1,0:T(8,128)(2,1)S(1)}, bf16[784,256]{1,0:T(8,128)(2,1)}, u32[]{:S(2)}) copy-start(bf16[784,256]{1,0:T(8,128)(2,1)} %constant.25.clone.tab) | copy-start | bytes 1204228
  26.0 1.3 %copy-start.3 = (bf16[3,2,8,144,128]{4,3,2,1,0:T(8,128)(2,1)}, bf16[3,2,8,144,128]{4,3,2,1,0:T(8,128)(2,1)S(1)}, u32[]{:S(2)}) copy-start(bf16[3,2,8,144,128]{4,3,2,1,0:T(8,128)(2,1)S(1)} %get-tuple-element.10.rest_0_.rest_1_.rest_2_) | copy-start | bytes 5308420
  27.7 1.5 %copy-start.4 = (bf16[3,2,8,144,128]{4,3,2,1,0:T(8,128)(2,1)S(1)}, bf16[3,2,8,144,128]{4,3,2,1,0:T(8,128)(2,1)}, u32[]{:S(2)}) copy-start(bf16[3,2,8,144,128]{4,3,2,1,0:T(8,128)(2,1)} %copy-done.3) | copy-start | bytes 5308420
